TPU v7x, 32 devices: a whole 2x2x4 slice. The times are simulated.
32 devices in a mesh: row: 4 (over x, core), col: 8 (over z, y).
Axes of the slice: x: 2, y: 2, z: 4, core: 2. Of those that a mesh axis runs over, the one named last changes fastest.
Arguments:
- ground_level_map: float32 [512, 4096], P('row', 'col'), may hold values from 0 to 10
- shoreline_altitude_entries: float32 [32768, 128], P(('row', 'col')), may hold values from 2 to 14
- shoreline_piece_position: int32 [32768], P(('row', 'col')), may hold values from 0 to 511
- lake_panel_locations: float32 [512, 2, 512], P(('row', 'col')), may hold values from 0 to 4096, as said below
- spanned_patch_verticals: int32 [512, 2], P(('row', 'col')), may hold values from 0 to 7, all different within a row; in each aligned block of 16 rows (0 to 15, 16 to 31, ...) at most 6 rows name the same one
Outputs:
- depth: float32 [512, 4096], P('row', 'col')
Inputs may be any that keep to these rules, and one draw needn't show every extreme that they name: shoreline_piece_position // 4 numbers a water body of the record's own tile row. `spanned_patch_verticals`: each body names 2 different tile columns; among the 16 bodies of one device no tile column is named more than 6 times, and some device's bodies name some column exactly 6 times. `lake_panel_locations`: entry 0 of a point is a row coordinate inside the rows of the body's tile row, entry 1 a column coordinate of the grid.
All inputs are finite; a program needn't handle non-finite values.
Results may differ from a plain program's by a relative error of at most 0.0003.
Values sent between devices are 32-bit elements; how exact they have to be, the bound alone decides.
No kernel may reach another device: no remote copies, remote signals or barrier semaphores. Data moves between devices by JAX's collectives and lax.ppermute only.
A program may use at most 64 MiB of HBM per device.

v0:
```python
import jax
import jax.numpy as jnp
from jax import lax
from jax.sharding import PartitionSpec as P

SEGS = 4
SWEEPS = 4


spread = 4.0
tau_weight = 4.0
flow_gain = 8.0
panel_block = 8


def extended(block, sides, width):
    for axis, dim in sides:
        count = lax.axis_size(axis)
        forward = [(i, i + 1) for i in range(count - 1)]
        backward = [(target, source) for source, target in forward]
        low = lax.ppermute(
            lax.slice_in_dim(block, block.shape[dim] - width, None, axis=dim), axis, forward
        )
        high = lax.ppermute(lax.slice_in_dim(block, 0, width, axis=dim), axis, backward)
        block = jnp.concatenate([low, block, high], axis=dim)
    return block


def conduct(depth_ext, ground_altitude, inside):
    center = depth_ext[1:-1, 1:-1]
    height = ground_altitude[1:-1, 1:-1]
    inside_here = inside[1:-1, 1:-1]
    weighted = center
    denominator = jnp.ones_like(center)
    for near_depth, near_height, near_inside in (
        (depth_ext[:-2, 1:-1], ground_altitude[:-2, 1:-1], inside[:-2, 1:-1]),
        (depth_ext[2:, 1:-1], ground_altitude[2:, 1:-1], inside[2:, 1:-1]),
        (depth_ext[1:-1, :-2], ground_altitude[1:-1, :-2], inside[1:-1, :-2]),
        (depth_ext[1:-1, 2:], ground_altitude[1:-1, 2:], inside[1:-1, 2:]),
    ):
        conduct_w = flow_gain * inside_here * near_inside / (1.0 + jnp.abs(height - near_height))
        weighted = weighted + conduct_w * near_depth
        denominator = denominator + conduct_w
    return weighted / denominator


def compact(panels, counts, covers, column):
    covering = jnp.any(covers == column, axis=1).astype(jnp.int32)
    ordering = jnp.argsort(1 - covering, stable=True)
    return (panels[ordering], counts[ordering], jnp.sum(covering))


def tile_water_surface(
    ordered_entries,
    ordered_tallies,
    flooded_tally,
    pixel_line_offset,
    vertical_offset,
    ground_altitude,
):
    patch_line_total, patch_vertical_total = ground_altitude.shape
    repeat_width = ordered_entries.shape[2] // ordered_tallies.shape[1]
    row_pos = (pixel_line_offset + jnp.arange(patch_line_total, dtype=jnp.int32)).astype(
        jnp.float32
    )
    col_pos = (vertical_offset + jnp.arange(patch_vertical_total, dtype=jnp.int32)).astype(
        jnp.float32
    )

    def add_block(block_id, accum):
        first_row = (block_id * panel_block).astype(jnp.int32)
        part_panels = lax.dynamic_slice_in_dim(ordered_entries, first_row, panel_block, 0)
        part_counts = lax.dynamic_slice_in_dim(ordered_tallies, first_row, panel_block, 0)
        live_rows = (first_row + jnp.arange(panel_block, dtype=jnp.int32) < flooded_tally).astype(
            jnp.float32
        )[:, None]
        elev_part = (part_panels[:, 0] * live_rows).reshape(-1)
        count_part = (jnp.repeat(part_counts, repeat_width, axis=1) * live_rows).reshape(-1)
        row_coord = part_panels[:, 1].reshape(-1)
        col_coord = part_panels[:, 2].reshape(-1)
        row_dist = (row_pos[:, None] - row_coord[None, :]) / spread
        col_dist = (col_pos[:, None] - col_coord[None, :]) / spread
        row_kernel = 1.0 / (1.0 + row_dist * row_dist)
        col_kernel = 1.0 / (1.0 + col_dist * col_dist)
        stacked = jnp.concatenate(
            [row_kernel * elev_part[None, :], row_kernel * count_part[None, :]], axis=0
        )
        return accum + lax.dot_general(
            stacked,
            col_kernel,
            (((1,), (1,)), ((), ())),
            precision=lax.Precision.HIGHEST,
            preferred_element_type=jnp.float32,
        )

    blocks = (flooded_tally + panel_block - 1) // panel_block
    accum = lax.fori_loop(
        0, blocks, add_block, jnp.zeros((2 * patch_line_total, patch_vertical_total), jnp.float32)
    )
    surface = (accum[:patch_line_total] + tau_weight * ground_altitude) / (
        accum[patch_line_total:] + tau_weight
    )
    return jnp.maximum(surface - ground_altitude, 0.0)


def inside_mask(
    pixel_line_offset,
    vertical_offset,
    patch_line_total,
    patch_vertical_total,
    margin,
    grid_rows,
    grid_cols,
):
    row_ids = (
        pixel_line_offset - margin + jnp.arange(patch_line_total + 2 * margin, dtype=jnp.int32)
    )
    col_ids = (
        vertical_offset - margin + jnp.arange(patch_vertical_total + 2 * margin, dtype=jnp.int32)
    )
    row_ok = (row_ids >= 0) & (row_ids < grid_rows)
    col_ok = (col_ids >= 0) & (col_ids < grid_cols)
    return (row_ok[:, None] & col_ok[None, :]).astype(jnp.float32)


def crop_edges(values, margin):
    return values[margin : values.shape[0] - margin, margin : values.shape[1] - margin]


def body(
    ground_level_map,
    shoreline_altitude_entries,
    shoreline_piece_position,
    lake_panel_locations,
    spanned_patch_verticals,
):
    patch_line_total, patch_vertical_total = ground_level_map.shape
    col_count = lax.axis_size("col")
    row_count = lax.axis_size("row")
    sample_width = shoreline_altitude_entries.shape[1]
    points = SEGS * sample_width
    body_count, cover_count = spanned_patch_verticals.shape
    bodies_row = body_count * col_count
    slots_row = SEGS * bodies_row
    elev_sums = jax.ops.segment_sum(
        shoreline_altitude_entries, shoreline_piece_position, num_segments=slots_row
    )
    edge_counts = jax.ops.segment_sum(
        jnp.ones(shoreline_piece_position.shape, jnp.float32),
        shoreline_piece_position,
        num_segments=slots_row,
    )
    owned_sums, owned_counts = (
        lax.psum_scatter(
            elev_sums.reshape(bodies_row, points), "col", scatter_dimension=0, tiled=True
        ),
        lax.psum_scatter(
            edge_counts.reshape(bodies_row, SEGS), "col", scatter_dimension=0, tiled=True
        ),
    )
    panels = jnp.concatenate([owned_sums[:, None, :], lake_panel_locations], axis=1)
    column = lax.axis_index("col")
    gathered, gathered_counts, gathered_covers = (
        lax.all_gather(panels, "col", axis=0, tiled=True),
        lax.all_gather(owned_counts, "col", axis=0, tiled=True),
        lax.all_gather(spanned_patch_verticals, "col", axis=0, tiled=True),
    )
    ordered_entries, ordered_tallies, flooded_tally = compact(
        gathered, gathered_counts, gathered_covers, column
    )
    pixel_line_offset = lax.axis_index("row") * patch_line_total
    vertical_offset = column * patch_vertical_total
    depth = tile_water_surface(
        ordered_entries,
        ordered_tallies,
        flooded_tally,
        pixel_line_offset,
        vertical_offset,
        ground_level_map,
    )
    grid_rows = patch_line_total * row_count
    grid_cols = patch_vertical_total * col_count
    stacked = jnp.stack([ground_level_map, depth])
    padded_depth_field = extended(stacked, (("row", 1), ("col", 2)), SWEEPS)
    ground_altitude = padded_depth_field[0]
    depth_ext = padded_depth_field[1]
    inside = inside_mask(
        pixel_line_offset,
        vertical_offset,
        patch_line_total,
        patch_vertical_total,
        SWEEPS,
        grid_rows,
        grid_cols,
    )
    for sweep_index in range(SWEEPS):
        depth_ext = conduct(
            depth_ext, crop_edges(ground_altitude, sweep_index), crop_edges(inside, sweep_index)
        )
    depth = depth_ext
    return depth


def solution(mesh):
    in_specs = (
        P("row", "col"),
        P(("row", "col"), None),
        P(("row", "col")),
        P(("row", "col"), None, None),
        P(("row", "col"), None),
    )
    out_specs = P("row", "col")
    return jax.shard_map(body, mesh=mesh, in_specs=in_specs, out_specs=out_specs, check_vma=False)
```

profile of v0, /device:TPU:5, one launch (start us, length us, event | category | flops | bytes accessed | tf_op | source)
XLA Modules:
  0.0 264.7 jit_solution(10587039994832515684)
XLA Ops:
  6.5 7.7 %scatter_custom_fusion.1 = f32[512]{0:T(512)S(1)} fusion(s32[1024]{0:T(1024)} %param.9, f32[1024]{0:T(1024)S(1)} %broadcast.97, f32[]{:T(128)} %constant.29.clone.1), kind=kCustom, calls=%fused_computation.178 | custom fusion | flops 1024 | bytes 2560 | tf_op jit(solution)/shard_map/scatter-add | solution.py:148
  14.3 0.7 reshape.58
  15.1 6.5 %scatter_custom_fusion = f32[512,128]{1,0:T(8,128)S(1)} fusion(s32[1024]{0:T(1024)} %param.9, f32[1024,128]{1,0:T(8,128)} %param.8, f32[]{:T(128)} %constant.29.clone.1), kind=kCustom, calls=%fused_computation.163 | custom fusion | flops 131072 | bytes 262656 | tf_op jit(solution)/shard_map/scatter-add | solution.py:145
  21.6 0.7 reshape.57
  22.3 13.8 %all-gather = s32[8,16,2]{1,2,0:T(2,128)S(1)} all-gather(s32[1,16,2]{1,2,0:T(2,128)} %bitcast.41), channel_id=1, replica_groups=mesh['row'=4,'col'=8] {'col'}, dimensions={0}, use_global_device_ids=true | all-gather | bytes 1152 | tf_op jit(solution)/shard_map/all_gather | solution.py:166
  36.2 0.7 convert_subtract_fusion
  37.7 0.9 copy.21
  38.6 2.6 sort.17
  41.2 34.4 %reduce-scatter.5.cloned.1.call-done = f32[16,4]{1,0:T(8,128)} async-done(((f32[128,4]{1,0:T(8,128)}), f32[16,4]{1,0:T(8,128)}) %reduce-scatter.5.cloned.1.call-update) | async-done | bytes 272 | tf_op jit(solution)/shard_map/reduce_scatter | solution.py:157
  75.6 0.8 copy.23
  76.4 19.8 %all-gather.1 = f32[8,16,4]{1,2,0:T(4,128)S(1)} all-gather(f32[1,16,4]{1,2,0:T(4,128)S(1)} %bitcast.40), channel_id=1, replica_groups=mesh['row'=4,'col'=8] {'col'}, dimensions={0}, use_global_device_ids=true | all-gather | bytes 2304 | tf_op jit(solution)/shard_map/all_gather | solution.py:165
  97.0 42.6 %reduce-scatter.3.cloned.1.call-done = f32[16,512]{1,0:T(8,128)} async-done(((f32[128,512]{1,0:T(8,128)}), f32[16,512]{1,0:T(8,128)}) %reduce-scatter.3.cloned.1.call-update) | async-done | bytes 32784 | tf_op jit(solution)/shard_map/reduce_scatter | solution.py:154
  139.6 0.8 pad_maximum_fusion.5
  140.4 25.3 %all_gather.10 = f32[128,3,512]{2,0,1:T(8,128)S(1)} all-gather(f32[16,3,512]{2,0,1:T(8,128)S(1)} %pad_maximum_fusion.5), channel_id=1, replica_groups=mesh['row'=4,'col'=8] {'col'}, dimensions={0}, use_global_device_ids=true | all-gather | bytes 884736 | tf_op jit(solution)/shard_map/all_gather | solution.py:164
  166.3 1.2 gather_fusion
  167.5 31.2 %while.11 = (s32[]{:T(128)}, f32[256,512]{1,0:T(8,128)S(1)}, s32[]{:T(128)}, f32[128,3,512]{2,1,0:T(4,128)S(1)}, s32[]{:T(128)}, /*index=5*/f32[128,4]{0,1:T(4,1...) while((s32[]{:T(128)}, f32[256,512]{1,0:T(8,128)S(1)}, ...), condition=%wide.region_8.9_spmd.clone, body=%wide.region_7.8_spmd.clone.sunk | while | flops 6457796096 | bytes 9754539 | solution.py:97
  168.0 0.7 compare_convert_fusion.2
  169.5 8.5 %fusion.112 = f32[256,512]{1,0:T(8,128)S(1)} fusion(f32[256,512]{1,0:T(8,128)S(1)} %get-tuple-element.215, f32[4096]{0:T(1024)S(1)} %bitcast.38, f32[512]{0:T(512)S(1)} %add_convert_fusion.4, f32[128,4096]{1,0:T(8,128)S(1)} %get-tuple-element.198, f32[128,4096]{1,0:T(8,128)S(1)} %get-tuple-element.199), kind=kOutput, calls=%fused_computation.22.clone.1 | convolution fusion | flops 6454116352 | bytes 5261312 | tf_op jit(solution)/shard_map/while/body/dot_general | solution.py:88
  178.4 0.7 compare_convert_fusion.2
  179.8 8.5 %fusion.112 = f32[256,512]{1,0:T(8,128)S(1)} fusion(f32[256,512]{1,0:T(8,128)S(1)} %get-tuple-element.215, f32[4096]{0:T(1024)S(1)} %bitcast.38, f32[512]{0:T(512)S(1)} %add_convert_fusion.4, f32[128,4096]{1,0:T(8,128)S(1)} %get-tuple-element.198, f32[128,4096]{1,0:T(8,128)S(1)} %get-tuple-element.199), kind=kOutput, calls=%fused_computation.22.clone.1 | convolution fusion | flops 6454116352 | bytes 5261312 | tf_op jit(solution)/shard_map/while/body/dot_general | solution.py:88
  188.7 0.7 compare_convert_fusion.2
  190.2 8.5 %fusion.112 = f32[256,512]{1,0:T(8,128)S(1)} fusion(f32[256,512]{1,0:T(8,128)S(1)} %get-tuple-element.215, f32[4096]{0:T(1024)S(1)} %bitcast.38, f32[512]{0:T(512)S(1)} %add_convert_fusion.4, f32[128,4096]{1,0:T(8,128)S(1)} %get-tuple-element.198, f32[128,4096]{1,0:T(8,128)S(1)} %get-tuple-element.199), kind=kOutput, calls=%fused_computation.22.clone.1 | convolution fusion | flops 6454116352 | bytes 5261312 | tf_op jit(solution)/shard_map/while/body/dot_general | solution.py:88
  198.9 10.6 %collective-permute-start = (f32[2,4,512]{2,1,0:T(4,128)S(1)}, f32[2,4,512]{2,1,0:T(4,128)S(1)}, u32[]{:S(2)}, u32[]{:S(2)}) collective-permute-start(f32[2,4,512]{2,1,0:T(4,128)S(1)} %get-tuple-element.132), channel_id=1, source_target_pairs={{0,8},{8,16},{16,24},{1,9},{9,17},{17,25},{2,10},{10,18},{18,26},{... | collective-permute-start | bytes 49160 | tf_op jit(solution)/shard_map/ppermute | solution.py:21
  209.5 1.9 collective-permute-start.1
  211.5 3.1 %collective-permute-done.1 = f32[2,4,512]{2,1,0:T(4,128)S(1)} collective-permute-done((f32[2,4,512]{2,1,0:T(4,128)S(1)}, f32[2,4,512]{2,1,0:T(4,128)S(1)}, u32[]{:S(2)}, u32[]{:S(2)}) %collective-permute-start.1) | collective-permute-done | bytes 16416 | tf_op jit(solution)/shard_map/ppermute | solution.py:24
  214.7 4.3 %collective-permute-start.2 = (f32[2,136,4]{2,1,0:T(8,128)S(1)}, f32[2,136,4]{2,1,0:T(8,128)S(1)}, u32[]{:S(2)}, u32[]{:S(2)}) collective-permute-start(f32[2,136,4]{2,1,0:T(8,128)S(1)} %get-tuple-element.130), channel_id=1, source_target_pairs={{0,1},{1,2},{2,3},{3,4},{4,5},{5,6},{6,7},{8,9},{9,10},{10,11},{11... | collective-permute-start | bytes 13064 | tf_op jit(solution)/shard_map/ppermute | solution.py:21
  219.0 12.9 %collective-permute-start.3 = (f32[2,136,4]{2,1,0:T(8,128)S(1)}, f32[2,136,4]{2,1,0:T(8,128)S(1)}, u32[]{:S(2)}, u32[]{:S(2)}) collective-permute-start(f32[2,136,4]{2,1,0:T(8,128)S(1)} %get-tuple-element.131), channel_id=1, source_target_pairs={{1,0},{2,1},{3,2},{4,3},{5,4},{6,5},{7,6},{9,8},{10,9},{11,10},{12... | collective-permute-start | bytes 13064 | tf_op jit(solution)/shard_map/ppermute | solution.py:24
  232.2 19.5 %collective-permute-done.3 = f32[2,136,4]{2,1,0:T(8,128)S(1)} collective-permute-done((f32[2,136,4]{2,1,0:T(8,128)S(1)}, f32[2,136,4]{2,1,0:T(8,128)S(1)}, u32[]{:S(2)}, u32[]{:S(2)}) %collective-permute-start.3) | collective-permute-done | bytes 4384 | tf_op jit(solution)/shard_map/ppermute | solution.py:24
  252.1 1.2 fusion.62
  253.3 1.4 fusion.45
  254.7 1.4 fusion.28
  256.1 1.7 fusion.79
  (57 shorter events, 5.6 us)
Async XLA Ops:
  6.5 69.1 %reduce-scatter.5.cloned.1.call-start = ((), (), s32[]{:S(2)}) async-start(), calls=%async_computation.3 | async-start | bytes 73728 | tf_op jit(solution)/shard_map/reduce_scatter | solution.py:157
  15.0 124.6 %reduce-scatter.3.cloned.1.call-start = ((), (), s32[]{:S(2)}) async-start(), calls=%async_computation.2 | async-start | bytes 294912 | tf_op jit(solution)/shard_map/reduce_scatter | solution.py:154
  167.5 31.2 %copy-start = (f32[128,512]{1,0:T(8,128)S(1)}, f32[128,512]{1,0:T(8,128)}, u32[]{:S(2)}) copy-start(f32[128,512]{1,0:T(8,128)} %param.7) | copy-start | bytes 786436
  198.9 12.6 %collective-permute-start = (f32[2,4,512]{2,1,0:T(4,128)S(1)}, f32[2,4,512]{2,1,0:T(4,128)S(1)}, u32[]{:S(2)}, u32[]{:S(2)}) collective-permute-start(f32[2,4,512]{2,1,0:T(4,128)S(1)} %get-tuple-element.132), channel_id=1, source_target_pairs={{0,8},{8,16},{16,24},{1,9},{9,17},{17,25},{2,10},{10,18},{18,26},{... | collective-permute-start | bytes 49160 | tf_op jit(solution)/shard_map/ppermute | solution.py:21
  209.5 5.1 %collective-permute-start.1 = (f32[2,4,512]{2,1,0:T(4,128)S(1)}, f32[2,4,512]{2,1,0:T(4,128)S(1)}, u32[]{:S(2)}, u32[]{:S(2)}) collective-permute-start(f32[2,4,512]{2,1,0:T(4,128)S(1)} %get-tuple-element.133), channel_id=1, source_target_pairs={{8,0},{16,8},{24,16},{9,1},{17,9},{25,17},{10,2},{18,10},{26,18},{... | collective-permute-start | bytes 49160 | tf_op jit(solution)/shard_map/ppermute | solution.py:24
  214.7 17.5 %collective-permute-start.2 = (f32[2,136,4]{2,1,0:T(8,128)S(1)}, f32[2,136,4]{2,1,0:T(8,128)S(1)}, u32[]{:S(2)}, u32[]{:S(2)}) collective-permute-start(f32[2,136,4]{2,1,0:T(8,128)S(1)} %get-tuple-element.130), channel_id=1, source_target_pairs={{0,1},{1,2},{2,3},{3,4},{4,5},{5,6},{6,7},{8,9},{9,10},{10,11},{11... | collective-permute-start | bytes 13064 | tf_op jit(solution)/shard_map/ppermute | solution.py:21
  219.0 32.7 %collective-permute-start.3 = (f32[2,136,4]{2,1,0:T(8,128)S(1)}, f32[2,136,4]{2,1,0:T(8,128)S(1)}, u32[]{:S(2)}, u32[]{:S(2)}) collective-permute-start(f32[2,136,4]{2,1,0:T(8,128)S(1)} %get-tuple-element.131), channel_id=1, source_target_pairs={{1,0},{2,1},{3,2},{4,3},{5,4},{6,5},{7,6},{9,8},{10,9},{11,10},{12... | collective-permute-start | bytes 13064 | tf_op jit(solution)/shard_map/ppermute | solution.py:24
Sparse Core Ops, SparseCore 0:
  15.2 60.4 reduce-scatter.4
  79.0 60.6 reduce-scatter.2
where the time goes:
time: 269 us; the launch traced here: 265 us
  waiting for transfers between devices  99.8 us (37%)
  blocking collectives  58.9 us (22%)
  starting transfers between devices  29.8 us (11%)
  other arithmetic  28.8 us (11%)
  matrix products  25.6 us (10%)
  between operations  14.3 us (5%)
  local copies, waits for them, and re-layouts  6.94 us (3%)
    reduce_scatter x1, waiting for transfers between devices, body(): lax.psum_scatter(elev_sums.reshape(bodies_row, points), 'col', scatter_di...  42.6 us
    reduce_scatter x1, waiting for transfers between devices, body(): lax.psum_scatter(edge_counts.reshape(bodies_row, SEGS), 'col', scatter_di...  34.4 us
    dot_general x3, matrix products, add_block(): lax.dot_general(stacked, col_kernel, (((1,), (1,)), ((), ())), precision=...  25.6 us
    all_gather x1, blocking collectives, body(): lax.all_gather(panels, 'col', axis=0, tiled=True)  25.3 us
    ppermute x2, waiting for transfers between devices, extended(): lax.ppermute(lax.slice_in_dim(block, 0, width, axis=dim), axis, backward)  22.6 us
    all_gather x1, blocking collectives, body(): lax.all_gather(owned_counts, 'col', axis=0, tiled=True)  19.8 us
    ppermute x2, starting transfers between devices, extended(): lax.ppermute(lax.slice_in_dim(block, block.shape[dim] - width, None, axis...  15 us
    ppermute x2, starting transfers between devices, extended(): lax.ppermute(lax.slice_in_dim(block, 0, width, axis=dim), axis, backward)  14.8 us
  transfers between devices with their start and end apart: 6, of which 5 were waited for; matrix products, arithmetic and copies ran while one was open for 5% of the time, Pallas kernels for 0%

commit v1 on v0

v1 whole, which is shorter than its diff:
```python
import functools

import jax
import jax.numpy as jnp
from jax import lax
from jax.experimental import pallas as pl
from jax.experimental.pallas import tpu as pltpu
from jax.sharding import PartitionSpec as P

SEGS = 4
SWEEPS = 4
MOST = 6
LANES = 128

spread = 4.0
tau_weight = 4.0
flow_gain = 8.0

F32 = jnp.float32
BF16 = jnp.bfloat16
VMEM_LIMIT = 48 * 1024 * 1024


def vmem():
    return pl.BlockSpec(memory_space=pltpu.VMEM)


def smem():
    return pl.BlockSpec(memory_space=pltpu.SMEM)


def params():
    return pltpu.CompilerParams(vmem_limit_bytes=VMEM_LIMIT)


def one_hot(cond):
    return jnp.where(cond, 1.0, 0.0).astype(BF16)


def segment_kernel(ids_ref, entry_ref, out_ref):
    owners, rows, _ = out_ref.shape
    bodies = rows // (SEGS + 1)
    chunks = ids_ref.shape[0]
    seg_iota = lax.broadcasted_iota(jnp.int32, (owners * bodies * SEGS, LANES), 0)
    body_iota = lax.broadcasted_iota(jnp.int32, (owners * bodies, LANES), 0)
    lane_seg = lax.broadcasted_iota(jnp.int32, (LANES, LANES), 0) // (LANES // SEGS)
    ids = [ids_ref[k : k + 1, :] for k in range(chunks)]
    by_segment = jnp.concatenate([one_hot(seg_iota == v) for v in ids], axis=1)
    by_body = jnp.concatenate([one_hot(body_iota == v // SEGS) for v in ids], axis=1)
    by_lane = jnp.concatenate([one_hot(lane_seg == v % SEGS) for v in ids], axis=1)
    entries = entry_ref[...]
    high = entries.astype(BF16)
    low = (entries - high.astype(F32)).astype(BF16)
    both = jnp.dot(
        by_segment, jnp.concatenate([high, low], axis=1), preferred_element_type=F32
    )
    sums = both[:, :LANES] + both[:, LANES:]
    counts = lax.dot_general(
        by_body, by_lane, (((1,), (1,)), ((), ())), preferred_element_type=F32
    )
    for owner in range(owners):
        step = bodies * SEGS
        out_ref[owner, :step, :] = sums[owner * step : (owner + 1) * step]
        out_ref[owner, step:, :] = counts[owner * bodies : (owner + 1) * bodies]


def locations_kernel(cover_ref, place_ref, out_ref, used_ref):
    columns = out_ref.shape[0]
    bodies, covers = cover_ref.shape
    out_ref[...] = jnp.zeros_like(out_ref)
    for column in range(columns):
        used_ref[column] = 0
    for body_id in range(bodies):
        rows = place_ref[body_id]
        tile = jnp.concatenate(
            [
                rows[axis : axis + 1, s * LANES : (s + 1) * LANES]
                for axis in range(2)
                for s in range(SEGS)
            ],
            axis=0,
        )
        for k in range(covers):
            column = cover_ref[body_id, k]
            slot = used_ref[column]
            used_ref[column] = slot + 1
            out_ref[column, slot] = tile


def owner_kernel(cover_ref, part_ref, out_ref, total_ref, used_ref):
    columns = out_ref.shape[0]
    bodies, covers = cover_ref.shape
    total = part_ref[0]
    for source in range(1, part_ref.shape[0]):
        total = total + part_ref[source]
    total_ref[...] = total
    out_ref[...] = jnp.zeros_like(out_ref)
    for column in range(columns):
        used_ref[column] = 0
    for body_id in range(bodies):
        sums = total_ref[body_id * SEGS : (body_id + 1) * SEGS, :]
        count = total_ref[bodies * SEGS + body_id : bodies * SEGS + body_id + 1, :]
        for k in range(covers):
            column = cover_ref[body_id, k]
            slot = used_ref[column]
            used_ref[column] = slot + 1
            out_ref[column, pl.ds(slot * SEGS, SEGS), :] = sums
            out_ref[column, pl.ds(MOST * SEGS + slot, 1), :] = count


def lorentz(size, origin, coord):
    shifted = (coord - origin) * (1.0 / spread)
    index = lax.broadcasted_iota(jnp.int32, (size, LANES), 0).astype(F32) * (1.0 / spread)
    distance = index - shifted
    return 1.0 / (1.0 + distance * distance)


def column_kernel(place_ref, out_ref):
    tile_columns = out_ref.shape[1]
    origin = (lax.axis_index("col") * tile_columns).astype(F32)

    @pl.loop(0, MOST)
    def _(slot):
        tile = place_ref[0, slot]
        for s in range(SEGS):
            value = lorentz(tile_columns, origin, tile[SEGS + s : SEGS + s + 1, :])
            out_ref[0, :, pl.ds(pl.multiple_of((slot * SEGS + s) * LANES, LANES), LANES)] = (
                value.astype(BF16)
            )


def surface_kernel(place_ref, sums_ref, column_ref, ground_ref, depth_ref, strip_ref, acc_ref, mean_ref):
    owner = pl.program_id(0)
    tile_rows, _ = ground_ref.shape
    origin = (lax.axis_index("row") * tile_rows).astype(F32)

    @pl.when(owner == 0)
    def _():
        acc_ref[...] = jnp.zeros_like(acc_ref)
        elev = jnp.sum(sums_ref[:, : MOST * SEGS, :], axis=0)
        count = jnp.sum(sums_ref[:, MOST * SEGS : MOST * SEGS + 8, :], axis=0)
        elev = jnp.sum(jnp.sum(elev, axis=0, keepdims=True), axis=1, keepdims=True)
        count = jnp.sum(jnp.sum(count, axis=0, keepdims=True), axis=1, keepdims=True)
        mean_ref[...] = jnp.broadcast_to(elev / jnp.maximum(count * SEGS, 1.0), mean_ref.shape)

    mean = mean_ref[0:1, :]
    for slot in range(MOST):
        tile = place_ref[0, slot]
        elev_parts, count_parts = [], []
        for s in range(SEGS):
            count = sums_ref[owner, MOST * SEGS + slot : MOST * SEGS + slot + 1, :]
            lane = s * (LANES // SEGS)
            count = jnp.broadcast_to(count[:, lane : lane + 1], (1, LANES))
            elev = sums_ref[owner, slot * SEGS + s : slot * SEGS + s + 1, :] - mean * count
            value = lorentz(tile_rows, origin, tile[s : s + 1, :])
            elev_parts.append((value * elev).astype(BF16))
            count_parts.append((value * count).astype(BF16))
        stacked = jnp.concatenate(
            [jnp.concatenate(elev_parts, axis=1), jnp.concatenate(count_parts, axis=1)], axis=0
        )
        points = SEGS * LANES
        acc_ref[...] += lax.dot_general(
            stacked,
            column_ref[0, :, slot * points : (slot + 1) * points],
            (((1,), (1,)), ((), ())),
            preferred_element_type=F32,
        )

    @pl.when(owner == pl.num_programs(0) - 1)
    def _():
        ground = ground_ref[...]
        den = acc_ref[tile_rows:, :]
        base = jnp.broadcast_to(mean_ref[0:1, 0:1], ground.shape)
        depth = (acc_ref[:tile_rows, :] + (base - ground) * den) / (den + tau_weight)
        depth = jnp.maximum(depth, 0.0)
        depth_ref[...] = depth
        strip_ref[...] = jnp.concatenate(
            [
                depth[:SWEEPS],
                depth[tile_rows - SWEEPS :],
                ground[:SWEEPS],
                ground[tile_rows - SWEEPS :],
            ],
            axis=0,
        )


def neighbour_rows(strip_ref, row_count):
    me = lax.axis_index("row")
    block = 4 * SWEEPS
    above = pl.multiple_of(jnp.maximum(me - 1, 0) * block, block)
    below = pl.multiple_of(jnp.minimum(me + 1, row_count - 1) * block, block)
    above = strip_ref[pl.ds(above, block), :]
    below = strip_ref[pl.ds(below, block), :]
    return (
        above[SWEEPS : 2 * SWEEPS],
        below[:SWEEPS],
        above[3 * SWEEPS :],
        below[2 * SWEEPS : 3 * SWEEPS],
    )


def edge_kernel(row_count, strip_ref, depth_ref, ground_ref, left_ref, right_ref):
    tile_rows, tile_columns = depth_ref.shape
    depth_up, depth_down, ground_up, ground_down = neighbour_rows(strip_ref, row_count)
    for out_ref, start, pick in (
        (left_ref, 0, 0),
        (right_ref, tile_columns - LANES, LANES - SWEEPS),
    ):
        lanes = slice(start, start + LANES)
        for k, (ref, up, down) in enumerate(
            ((depth_ref, depth_up, depth_down), (ground_ref, ground_up, ground_down))
        ):
            main = jnp.transpose(ref[:, lanes])[pick : pick + SWEEPS]
            outer = jnp.concatenate([up[:, lanes], down[:, lanes]], axis=0)
            outer = jnp.transpose(outer)[pick : pick + SWEEPS]
            out_ref[k * SWEEPS : (k + 1) * SWEEPS, :tile_rows] = main
            out_ref[k * SWEEPS : (k + 1) * SWEEPS, tile_rows:] = jnp.concatenate(
                [outer, jnp.zeros((SWEEPS, LANES - 2 * SWEEPS), F32)], axis=1
            )


def sweep_kernel(
    row_count, col_count, strip_ref, left_ref, right_ref, depth_ref, ground_ref, out_ref, height_ref, land_ref
):
    tile_rows, tile_columns = depth_ref.shape
    pad_rows, pad_cols = 8, LANES
    rows, cols = height_ref.shape
    depth_up, depth_down, ground_up, ground_down = neighbour_rows(strip_ref, row_count)
    for ref, inner_ref, up, down, k in (
        (height_ref, depth_ref, depth_up, depth_down, 0),
        (land_ref, ground_ref, ground_up, ground_down, SWEEPS),
    ):
        ref[...] = jnp.zeros_like(ref)
        inner = slice(pad_cols, pad_cols + tile_columns)
        ref[pad_rows : pad_rows + tile_rows, inner] = inner_ref[...]
        ref[pad_rows - SWEEPS : pad_rows, inner] = up
        ref[pad_rows + tile_rows : pad_rows + tile_rows + SWEEPS, inner] = down
        for side_ref, first in (
            (left_ref, pad_cols - SWEEPS),
            (right_ref, pad_cols + tile_columns),
        ):
            main = jnp.transpose(side_ref[:, :tile_rows])[:, k : k + SWEEPS]
            outer = jnp.transpose(side_ref[:, tile_rows:])[: 2 * SWEEPS, k : k + SWEEPS]
            lanes = slice(first, first + SWEEPS)
            ref[pad_rows : pad_rows + tile_rows, lanes] = main
            ref[pad_rows - SWEEPS : pad_rows, lanes] = outer[:SWEEPS]
            ref[pad_rows + tile_rows : pad_rows + tile_rows + SWEEPS, lanes] = outer[SWEEPS:]

    row_id = lax.broadcasted_iota(jnp.int32, (rows, cols), 0) + (
        lax.axis_index("row") * tile_rows - pad_rows
    )
    col_id = lax.broadcasted_iota(jnp.int32, (rows, cols), 1) + (
        lax.axis_index("col") * tile_columns - pad_cols
    )
    grid_rows, grid_cols = tile_rows * row_count, tile_columns * col_count
    land = land_ref[...]
    down = flow_gain / (1.0 + jnp.abs(land - pltpu.roll(land, rows - 1, 0)))
    right = flow_gain / (1.0 + jnp.abs(land - pltpu.roll(land, cols - 1, 1)))
    down = jnp.where((row_id >= 0) & (row_id < grid_rows - 1), down, 0.0)
    right = jnp.where((col_id >= 0) & (col_id < grid_cols - 1), right, 0.0)
    up = pltpu.roll(down, 1, 0)
    left = pltpu.roll(right, 1, 1)
    scale = 1.0 / (1.0 + up + down + left + right)
    up, down, left, right = up * scale, down * scale, left * scale, right * scale
    height = height_ref[...]
    for _ in range(SWEEPS):
        height = (
            height * scale
            + up * pltpu.roll(height, 1, 0)
            + down * pltpu.roll(height, rows - 1, 0)
            + left * pltpu.roll(height, 1, 1)
            + right * pltpu.roll(height, cols - 1, 1)
        )
    out_ref[...] = height[pad_rows : pad_rows + tile_rows, pad_cols : pad_cols + tile_columns]


def shift(values, axis, step):
    count = lax.axis_size(axis)
    return lax.ppermute(values, axis, [(i, (i + step) % count) for i in range(count)])


def body(
    ground_level_map,
    shoreline_altitude_entries,
    shoreline_piece_position,
    lake_panel_locations,
    spanned_patch_verticals,
):
    tile_rows, tile_columns = ground_level_map.shape
    col_count = lax.axis_size("col")
    row_count = lax.axis_size("row")
    records, _ = shoreline_altitude_entries.shape
    bodies, _ = spanned_patch_verticals.shape
    covers = spanned_patch_verticals
    points = SEGS * LANES

    places = pl.pallas_call(
        locations_kernel,
        out_shape=jax.ShapeDtypeStruct((col_count, MOST, 2 * SEGS, LANES), F32),
        in_specs=[smem(), vmem()],
        out_specs=vmem(),
        scratch_shapes=[pltpu.SMEM((col_count,), jnp.int32)],
        compiler_params=params(),
    )(covers, lake_panel_locations)
    places = lax.all_to_all(places, "col", 0, 0, tiled=True)

    parts = pl.pallas_call(
        segment_kernel,
        out_shape=jax.ShapeDtypeStruct((col_count, bodies * (SEGS + 1), LANES), F32),
        in_specs=[vmem(), vmem()],
        out_specs=vmem(),
        compiler_params=params(),
    )(shoreline_piece_position.reshape(records // LANES, LANES), shoreline_altitude_entries)
    parts = lax.all_to_all(parts, "col", 0, 0, tiled=True)

    column_kernels = pl.pallas_call(
        column_kernel,
        grid=(col_count,),
        out_shape=jax.ShapeDtypeStruct((col_count, tile_columns, MOST * points), BF16),
        in_specs=[pl.BlockSpec((1, MOST, 2 * SEGS, LANES), lambda o: (o, 0, 0, 0))],
        out_specs=pl.BlockSpec((1, tile_columns, MOST * points), lambda o: (o, 0, 0)),
        compiler_params=params(),
        cost_estimate=pl.CostEstimate(
            flops=8 * col_count * tile_columns * MOST * points,
            transcendentals=0,
            bytes_accessed=2 * col_count * tile_columns * MOST * points,
        ),
    )(places)

    slot_rows = MOST * SEGS + 8
    sums = pl.pallas_call(
        owner_kernel,
        out_shape=jax.ShapeDtypeStruct((col_count, slot_rows, LANES), F32),
        in_specs=[smem(), vmem()],
        out_specs=vmem(),
        scratch_shapes=[
            pltpu.VMEM((bodies * (SEGS + 1), LANES), F32),
            pltpu.SMEM((col_count,), jnp.int32),
        ],
        compiler_params=params(),
    )(covers, parts)
    sums = lax.all_to_all(sums, "col", 0, 0, tiled=True)

    depth, strips = pl.pallas_call(
        surface_kernel,
        grid=(col_count,),
        out_shape=(
            jax.ShapeDtypeStruct((tile_rows, tile_columns), F32),
            jax.ShapeDtypeStruct((4 * SWEEPS, tile_columns), F32),
        ),
        in_specs=[
            pl.BlockSpec((1, MOST, 2 * SEGS, LANES), lambda o: (o, 0, 0, 0)),
            pl.BlockSpec((col_count, slot_rows, LANES), lambda o: (0, 0, 0)),
            pl.BlockSpec((1, tile_columns, MOST * points), lambda o: (o, 0, 0)),
            pl.BlockSpec((tile_rows, tile_columns), lambda o: (0, 0)),
        ],
        out_specs=(
            pl.BlockSpec((tile_rows, tile_columns), lambda o: (0, 0)),
            pl.BlockSpec((4 * SWEEPS, tile_columns), lambda o: (0, 0)),
        ),
        scratch_shapes=[
            pltpu.VMEM((2 * tile_rows, tile_columns), F32),
            pltpu.VMEM((8, LANES), F32),
        ],
        compiler_params=params(),
    )(places, sums, column_kernels, ground_level_map)

    strips = lax.all_gather(strips, "row", axis=0, tiled=True)
    edge_shape = jax.ShapeDtypeStruct((2 * SWEEPS, tile_rows + LANES), F32)
    left, right = pl.pallas_call(
        functools.partial(edge_kernel, row_count),
        out_shape=(edge_shape, edge_shape),
        in_specs=[vmem()] * 3,
        out_specs=(vmem(), vmem()),
        compiler_params=params(),
    )(strips, depth, ground_level_map)
    from_left = shift(right, "col", 1)
    from_right = shift(left, "col", -1)

    scratch = pltpu.VMEM((tile_rows + 16, tile_columns + 2 * LANES), F32)
    return pl.pallas_call(
        functools.partial(sweep_kernel, row_count, col_count),
        out_shape=jax.ShapeDtypeStruct((tile_rows, tile_columns), F32),
        in_specs=[vmem()] * 5,
        out_specs=vmem(),
        scratch_shapes=[scratch, scratch],
        compiler_params=params(),
    )(strips, from_left, from_right, depth, ground_level_map)


def solution(mesh):
    in_specs = (
        P("row", "col"),
        P(("row", "col"), None),
        P(("row", "col")),
        P(("row", "col"), None, None),
        P(("row", "col"), None),
    )
    out_specs = P("row", "col")
    return jax.shard_map(body, mesh=mesh, in_specs=in_specs, out_specs=out_specs, check_vma=False)
```

time: 269 us -> 79.8 us (0.30)
  the two profiles are of different devices: /device:TPU:5 before, /device:TPU:0 now
where the time goes in v1:
time: 79.8 us; the launch traced here: 79.1 us
  Pallas kernels  36.1 us (45%)
  starting transfers between devices  19 us (24%)
  waiting for transfers between devices  15.2 us (19%)
  blocking collectives  5.43 us (7%)
  local copies, waits for them, and re-layouts  3.37 us (4%)
    pallas_call x1, Pallas kernels, body(): pl.pallas_call(column_kernel, grid=(col_count,), out_shape=jax.ShapeDtype...  15.3 us
    pallas_call x1, Pallas kernels, body(): pl.pallas_call(surface_kernel, grid=(col_count,), out_shape=(jax.ShapeDty...  14.1 us
    all_to_all x1, starting transfers between devices, body(): parts = lax.all_to_all(parts, 'col', 0, 0, tiled=True)  7.28 us
    all_to_all x1, waiting for transfers between devices, body(): parts = lax.all_to_all(parts, 'col', 0, 0, tiled=True)  7.23 us
    all_to_all x1, waiting for transfers between devices, body(): places = lax.all_to_all(places, 'col', 0, 0, tiled=True)  6.32 us
    all_gather x1, blocking collectives, body(): strips = lax.all_gather(strips, 'row', axis=0, tiled=True)  5.43 us
    ppermute x2, starting transfers between devices, shift(): lax.ppermute(values, axis, [(i, (i + step) % count) for i in range(count)])  4.78 us
    all_to_all x1, starting transfers between devices, body(): places = lax.all_to_all(places, 'col', 0, 0, tiled=True)  3.59 us
  transfers between devices with their start and end apart: 5, of which 3 were waited for; matrix products, arithmetic and copies ran while one was open for 1% of the time, Pallas kernels for 23%

profile of v1, /device:TPU:0, one launch (start us, length us, event | category | flops | bytes accessed | tf_op | source)
XLA Modules:
  0.0 79.1 jit_solution(12858085168632609654)
XLA Ops:
  0.0 0.0 copy-start
  0.0 0.0 copy-start.1
  0.0 1.1 %copy-done.1 = f32[1024,128]{1,0:T(8,128)S(1)} copy-done((f32[1024,128]{1,0:T(8,128)S(1)}, f32[1024,128]{1,0:T(8,128)}, u32[]{:S(2)}) %copy-start.1) | copy-done | bytes 524312
  1.1 0.0 copy-start.3
  1.1 0.7 copy-done.3
  1.8 1.2 %shard_map.56 = f32[8,80,128]{2,1,0:T(8,128)} custom-call(s32[8,128]{1,0:T(8,128)S(1)} %bitcast.1, f32[1024,128]{1,0:T(8,128)S(1)} %copy-done.1), custom_call_target="tpu_custom_call" | custom-call | tf_op jit(solution)/shard_map/pallas_call | solution.py:308
  3.0 7.3 %all-to-all-start.1 = ((f32[8,80,128]{2,1,0:T(8,128)}), f32[8,80,128]{2,1,0:T(8,128)S(1)}, u32[]{:S(2)}, u32[]{:S(2)}) async-start(f32[8,80,128]{2,1,0:T(8,128)} %shard_map.56), calls=%async_computation.1 | async-start | bytes 655360 | tf_op jit(solution)/shard_map/all_to_all | solution.py:315
  10.3 0.8 copy.6.cover_ref
  11.0 0.0 copy-start.2
  11.0 0.8 %copy-done.2 = f32[16,2,512]{2,1,0:T(2,128)S(1)} copy-done((f32[16,2,512]{2,1,0:T(2,128)S(1)}, f32[16,2,512]{2,1,0:T(2,128)}, u32[]{:S(2)}) %copy-start.2) | copy-done | bytes 65560
  11.9 1.5 %shard_map.55 = f32[8,6,8,128]{3,2,1,0:T(8,128)} custom-call(s32[16,2]{1,0:T(8,128)S(1)} %copy.6.cover_ref, f32[16,2,512]{2,1,0:T(2,128)S(1)} %copy-done.2), custom_call_target="tpu_custom_call" | custom-call | tf_op jit(solution)/shard_map/pallas_call | solution.py:298
  13.4 7.2 %all-to-all-done.1.part_ref = f32[8,80,128]{2,1,0:T(8,128)S(1)} async-done(((f32[8,80,128]{2,1,0:T(8,128)}), f32[8,80,128]{2,1,0:T(8,128)S(1)}, u32[]{:S(2)}, u32[]{:S(2)}) %all-to-all-start.1) | async-done | bytes 327712 | tf_op jit(solution)/shard_map/all_to_all | solution.py:315
  20.6 3.6 %all-to-all-start = ((f32[8,6,8,128]{3,2,1,0:T(8,128)}), f32[8,6,8,128]{3,2,1,0:T(8,128)S(1)}, u32[]{:S(2)}, u32[]{:S(2)}) async-start(f32[8,6,8,128]{3,2,1,0:T(8,128)} %shard_map.55), calls=%async_computation | async-start | bytes 393216 | tf_op jit(solution)/shard_map/all_to_all | solution.py:306
  24.2 1.5 %shard_map.57 = f32[8,32,128]{2,1,0:T(8,128)} custom-call(s32[16,2]{1,0:T(8,128)S(1)} %copy.6.cover_ref, f32[8,80,128]{2,1,0:T(8,128)S(1)} %all-to-all-done.1.part_ref), custom_call_target="tpu_custom_call" | custom-call | tf_op jit(solution)/shard_map/pallas_call | solution.py:332
  25.7 6.3 %all-to-all-done.place_ref = f32[8,6,8,128]{3,2,1,0:T(8,128)S(1)} async-done(((f32[8,6,8,128]{3,2,1,0:T(8,128)}), f32[8,6,8,128]{3,2,1,0:T(8,128)S(1)}, u32[]{:S(2)}, u32[]{:S(2)}) %all-to-all-start) | async-done | bytes 196640 | tf_op jit(solution)/shard_map/all_to_all | solution.py:306
  32.0 3.4 %all-to-all-start.2 = ((f32[8,32,128]{2,1,0:T(8,128)}), f32[8,32,128]{2,1,0:T(8,128)S(1)}, u32[]{:S(2)}, u32[]{:S(2)}) async-start(f32[8,32,128]{2,1,0:T(8,128)} %shard_map.57), calls=%async_computation.2 | async-start | bytes 262144 | tf_op jit(solution)/shard_map/all_to_all | solution.py:343
  35.4 15.3 %shard_map.58.column_ref = bf16[8,512,3072]{2,1,0:T(8,128)(2,1)} custom-call(f32[8,6,8,128]{3,2,1,0:T(8,128)S(1)} %all-to-all-done.place_ref), custom_call_target="tpu_custom_call" | custom-call | flops 100663296 | bytes 25165824 | tf_op jit(solution)/shard_map/pallas_call | solution.py:317
  50.7 0.0 all-to-all-done.2.sums_ref
  50.7 0.0 copy-done
  50.7 14.1 %shard_map.59 = (f32[128,512]{1,0:T(8,128)S(1)}, f32[16,512]{1,0:T(8,128)S(1)}) custom-call(f32[8,6,8,128]{3,2,1,0:T(8,128)S(1)} %all-to-all-done.place_ref, f32[8,32,128]{2,1,0:T(8,128)S(1)} %all-to-all-done.2.sums_ref, bf16[8,512,3072]{2,1,0:T(8,128)(2,1)} %shard_map.58.column_ref, f32[128,512]{1,0:T(8,128)S(1)} %copy-done), custom_call_target="tpu_custom_call" | custom-call | tf_op jit(solution)/shard_map/pallas_call | solution.py:345
  64.7 5.4 %all_gather.3.strip_ref = f32[64,512]{1,0:T(8,128)S(1)} all-gather(f32[16,512]{1,0:T(8,128)S(1)} %get-tuple-element.9), channel_id=1, replica_groups=mesh['row'=4,'col'=8] {'row'}, dimensions={0}, use_global_device_ids=true | all-gather | bytes 163840 | tf_op jit(solution)/shard_map/all_gather | solution.py:369
  70.2 0.2 shard_map.60
  70.3 1.9 %collective-permute-start = (f32[8,256]{1,0:T(8,128)S(1)}, f32[8,256]{1,0:T(8,128)S(1)}, u32[]{:S(2)}, u32[]{:S(2)}) collective-permute-start(f32[8,256]{1,0:T(8,128)S(1)} %get-tuple-element.11), channel_id=1, source_target_pairs={{0,1},{1,2},{2,3},{3,4},{4,5},{5,6},{6,7},{7,0},{8,9},{9,10},{10,1... | collective-permute-start | bytes 24584 | tf_op jit(solution)/shard_map/ppermute | solution.py:280
  72.3 2.8 %collective-permute-start.1 = (f32[8,256]{1,0:T(8,128)S(1)}, f32[8,256]{1,0:T(8,128)S(1)}, u32[]{:S(2)}, u32[]{:S(2)}) collective-permute-start(f32[8,256]{1,0:T(8,128)S(1)} %get-tuple-element.12), channel_id=1, source_target_pairs={{0,7},{1,0},{2,1},{3,2},{4,3},{5,4},{6,5},{7,6},{8,15},{9,8},{10,9... | collective-permute-start | bytes 24584 | tf_op jit(solution)/shard_map/ppermute | solution.py:280
  75.1 1.6 %collective-permute-done.left_ref = f32[8,256]{1,0:T(8,128)S(1)} collective-permute-done((f32[8,256]{1,0:T(8,128)S(1)}, f32[8,256]{1,0:T(8,128)S(1)}, u32[]{:S(2)}, u32[]{:S(2)}) %collective-permute-start) | collective-permute-done | bytes 8224 | tf_op jit(solution)/shard_map/ppermute | solution.py:280
  76.7 0.0 collective-permute-done.1.right_ref
  76.7 2.4 %shard_map.61 = f32[128,512]{1,0:T(8,128)} custom-call(f32[64,512]{1,0:T(8,128)S(1)} %all_gather.3.strip_ref, f32[8,256]{1,0:T(8,128)S(1)} %collective-permute-done.left_ref, f32[8,256]{1,0:T(8,128)S(1)} %collective-permute-done.1.right_ref, f32[128,512]{1,0:T(8,128)S(1)} %get-tuple-element.10.depth_ref, f32[128,512]{1,0:T(8,128)S(1)} %copy-done), custom_call_target="tpu_custom_call" | custom-call | tf_op jit(solution)/shard_map/pallas_call | solution.py:382
Async XLA Ops:
  0.0 50.7 %copy-start = (f32[128,512]{1,0:T(8,128)S(1)}, f32[128,512]{1,0:T(8,128)}, u32[]{:S(2)}) copy-start(f32[128,512]{1,0:T(8,128)} %ground_ref.5) | copy-start | bytes 786436
  0.0 1.1 %copy-start.1 = (f32[1024,128]{1,0:T(8,128)S(1)}, f32[1024,128]{1,0:T(8,128)}, u32[]{:S(2)}) copy-start(f32[1024,128]{1,0:T(8,128)} %entry_ref.1) | copy-start | bytes 1572868
  1.1 0.7 copy-start.3
  3.0 17.6 %all-to-all-start.1 = ((f32[8,80,128]{2,1,0:T(8,128)}), f32[8,80,128]{2,1,0:T(8,128)S(1)}, u32[]{:S(2)}, u32[]{:S(2)}) async-start(f32[8,80,128]{2,1,0:T(8,128)} %shard_map.56), calls=%async_computation.1 | async-start | bytes 655360 | tf_op jit(solution)/shard_map/all_to_all | solution.py:315
  11.0 0.8 %copy-start.2 = (f32[16,2,512]{2,1,0:T(2,128)S(1)}, f32[16,2,512]{2,1,0:T(2,128)}, u32[]{:S(2)}) copy-start(f32[16,2,512]{2,1,0:T(2,128)} %place_ref.1) | copy-start | bytes 196612
  20.6 11.4 %all-to-all-start = ((f32[8,6,8,128]{3,2,1,0:T(8,128)}), f32[8,6,8,128]{3,2,1,0:T(8,128)S(1)}, u32[]{:S(2)}, u32[]{:S(2)}) async-start(f32[8,6,8,128]{3,2,1,0:T(8,128)} %shard_map.55), calls=%async_computation | async-start | bytes 393216 | tf_op jit(solution)/shard_map/all_to_all | solution.py:306
  32.0 18.7 %all-to-all-start.2 = ((f32[8,32,128]{2,1,0:T(8,128)}), f32[8,32,128]{2,1,0:T(8,128)S(1)}, u32[]{:S(2)}, u32[]{:S(2)}) async-start(f32[8,32,128]{2,1,0:T(8,128)} %shard_map.57), calls=%async_computation.2 | async-start | bytes 262144 | tf_op jit(solution)/shard_map/all_to_all | solution.py:343
  70.3 6.4 %collective-permute-start = (f32[8,256]{1,0:T(8,128)S(1)}, f32[8,256]{1,0:T(8,128)S(1)}, u32[]{:S(2)}, u32[]{:S(2)}) collective-permute-start(f32[8,256]{1,0:T(8,128)S(1)} %get-tuple-element.11), channel_id=1, source_target_pairs={{0,1},{1,2},{2,3},{3,4},{4,5},{5,6},{6,7},{7,0},{8,9},{9,10},{10,1... | collective-permute-start | bytes 24584 | tf_op jit(solution)/shard_map/ppermute | solution.py:280
  72.3 4.5 %collective-permute-start.1 = (f32[8,256]{1,0:T(8,128)S(1)}, f32[8,256]{1,0:T(8,128)S(1)}, u32[]{:S(2)}, u32[]{:S(2)}) collective-permute-start(f32[8,256]{1,0:T(8,128)S(1)} %get-tuple-element.12), channel_id=1, source_target_pairs={{0,7},{1,0},{2,1},{3,2},{4,3},{5,4},{6,5},{7,6},{8,15},{9,8},{10,9... | collective-permute-start | bytes 24584 | tf_op jit(solution)/shard_map/ppermute | solution.py:280

commit v2 on v1

v2 whole, which is shorter than its diff:
```python
import functools

import jax
import jax.numpy as jnp
from jax import lax
from jax.experimental import pallas as pl
from jax.experimental.pallas import tpu as pltpu
from jax.sharding import PartitionSpec as P

SEGS = 4
SWEEPS = 4
MOST = 6
LANES = 128

spread = 4.0
tau_weight = 4.0
flow_gain = 8.0

F32 = jnp.float32
BF16 = jnp.bfloat16
VMEM_LIMIT = 24 * 1024 * 1024


def vmem():
    return pl.BlockSpec(memory_space=pltpu.VMEM)


def smem():
    return pl.BlockSpec(memory_space=pltpu.SMEM)


def params(limit=VMEM_LIMIT):
    return pltpu.CompilerParams(vmem_limit_bytes=limit)


def one_hot(cond):
    return jnp.where(cond, 1.0, 0.0).astype(BF16)


def pack_kernel(cover_ref, ids_hbm, entry_hbm, place_hbm, out_ref, ids_ref, entry_ref, place_ref, used_ref, sems):
    owners, _, _ = out_ref.shape
    covers, bodies = cover_ref.shape
    copies = [
        pltpu.make_async_copy(source, target, sems.at[k])
        for k, (source, target) in enumerate(
            ((ids_hbm, ids_ref), (entry_hbm, entry_ref), (place_hbm, place_ref))
        )
    ]
    for copy in copies:
        copy.start()
    chunks = ids_ref.shape[0]
    sum_rows, count_rows = bodies * SEGS, bodies // 2
    first_slot = sum_rows + count_rows
    out_ref[:, first_slot:, :] = jnp.zeros((owners, MOST * 8, LANES), F32)
    copies[0].wait()
    seg_iota = lax.broadcasted_iota(jnp.int32, (owners * sum_rows, LANES), 0)
    pair_iota = lax.broadcasted_iota(jnp.int32, (owners * count_rows, LANES), 0)
    lane_group = lax.broadcasted_iota(jnp.int32, (LANES, LANES), 0) // 16
    ids = [ids_ref[k : k + 1, :] for k in range(chunks)]
    by_pair = jnp.concatenate([one_hot(pair_iota == v // 8) for v in ids], axis=1)
    by_lane = jnp.concatenate([one_hot(lane_group == v % 8) for v in ids], axis=1)
    counts = lax.dot_general(
        by_pair, by_lane, (((1,), (1,)), ((), ())), preferred_element_type=F32
    )
    by_segment = jnp.concatenate([one_hot(seg_iota == v) for v in ids], axis=1)
    copies[1].wait()
    entries = entry_ref[...]
    high = entries.astype(BF16)
    low = (entries - high.astype(F32)).astype(BF16)
    both = jnp.dot(
        by_segment, jnp.concatenate([high, low], axis=1), preferred_element_type=F32
    )
    sums = both[:, :LANES] + both[:, LANES:]
    for owner in range(owners):
        out_ref[owner, :sum_rows, :] = sums[owner * sum_rows : (owner + 1) * sum_rows]
        out_ref[owner, sum_rows:first_slot, :] = counts[
            owner * count_rows : (owner + 1) * count_rows
        ]
    copies[2].wait()
    for column in range(owners):
        used_ref[column] = 0
    for body_id in range(bodies):
        rows = place_ref[body_id]
        tile = jnp.concatenate(
            [
                rows[axis : axis + 1, s * LANES : (s + 1) * LANES]
                for axis in range(2)
                for s in range(SEGS)
            ],
            axis=0,
        )
        for k in range(covers):
            column = cover_ref[k, body_id]
            slot = used_ref[column]
            used_ref[column] = slot + 1
            out_ref[column, pl.ds(pl.multiple_of(first_slot + slot * 8, 8), 8), :] = tile


def owner_kernel(cover_ref, part_ref, out_ref, total_ref, used_ref):
    columns = out_ref.shape[0]
    covers, bodies = cover_ref.shape
    rows = total_ref.shape[0]
    total = part_ref[0, :rows, :]
    for source in range(1, part_ref.shape[0]):
        total = total + part_ref[source, :rows, :]
    total_ref[...] = total
    out_ref[...] = jnp.zeros_like(out_ref)
    for column in range(columns):
        used_ref[column] = 0
    for body_id in range(bodies):
        sums = total_ref[body_id * SEGS : (body_id + 1) * SEGS, :]
        row, lane = bodies * SEGS + body_id // 2, 64 * (body_id % 2)
        count = total_ref[row : row + 1, lane : lane + 64]
        for k in range(covers):
            column = cover_ref[k, body_id]
            slot = used_ref[column]
            used_ref[column] = slot + 1
            out_ref[column, pl.ds(slot * SEGS, SEGS), :] = sums
            out_ref[column, pl.ds(MOST * SEGS + slot, 1), :64] = count


def lorentz(base, step):
    distance = base + step
    return 1.0 / (1.0 + distance * distance)


def cell_base(origin, coord):
    index = lax.broadcasted_iota(jnp.int32, (16, LANES), 0).astype(F32) * (1.0 / spread)
    return index - (coord - origin) * (1.0 / spread)


def column_block(place_ref, owner, row, origin, starts):
    parts = []
    for s in range(SEGS):
        base = cell_base(origin, place_ref[owner, row + SEGS + s : row + SEGS + s + 1, :])
        parts.append(
            jnp.concatenate(
                [
                    lorentz(base, (start + j) / spread).astype(BF16)
                    for start in starts
                    for j in range(0, LANES, 16)
                ],
                axis=0,
            )
        )
    return jnp.concatenate(parts, axis=1)


def times_stack(columns, stack):
    return lax.dot_general(
        columns, stack, (((1,), (1,)), ((), ())), preferred_element_type=F32
    )


def surface(acc, mean, ground):
    tile_rows = ground.shape[0]
    num = jnp.transpose(acc[:, :tile_rows])
    den = jnp.transpose(acc[:, tile_rows:])
    depth = (num + (mean - ground) * den) / (den + tau_weight)
    return jnp.maximum(depth, 0.0)


def outer_kernel(
    first_slot, place_ref, sums_ref, ground_ref, depth_ref, left_ref, right_ref, stack_ref, mean_ref, acc_ref
):
    tile_rows, tile_columns = ground_ref.shape
    owners = sums_ref.shape[0]
    row_origin = (lax.axis_index("row") * tile_rows).astype(F32)
    col_origin = (lax.axis_index("col") * tile_columns).astype(F32)
    elev = jnp.sum(sums_ref[:, : MOST * SEGS, :], axis=0)
    count = jnp.sum(sums_ref[:, MOST * SEGS : MOST * SEGS + 8, :], axis=0)
    elev = jnp.sum(jnp.sum(elev, axis=0, keepdims=True), axis=1, keepdims=True)
    count = jnp.sum(jnp.sum(count, axis=0, keepdims=True), axis=1, keepdims=True)
    mean = elev / jnp.maximum(count * (LANES / 16), 1.0)
    mean_ref[...] = jnp.broadcast_to(mean, mean_ref.shape)
    acc_ref[...] = jnp.zeros_like(acc_ref)
    starts = (0, tile_columns - LANES)

    @pl.loop(0, owners)
    def _(owner):
        for slot in range(MOST):
            row = first_slot + slot * 8
            blocks = []
            for s in range(SEGS):
                here = sums_ref[owner, MOST * SEGS + slot : MOST * SEGS + slot + 1, s * 16 : s * 16 + 1]
                part = sums_ref[owner, slot * SEGS + s : slot * SEGS + s + 1, :] - mean * here
                weight = jnp.broadcast_to(here, (16, LANES))
                part = jnp.broadcast_to(part, (16, LANES))
                base = cell_base(row_origin, place_ref[owner, row + s : row + s + 1, :])
                values = [lorentz(base, i / spread) for i in range(0, tile_rows, 16)]
                block = jnp.concatenate(
                    [(v * part).astype(BF16) for v in values]
                    + [(v * weight).astype(BF16) for v in values],
                    axis=0,
                )
                stack_ref[owner * (MOST * SEGS) + slot * SEGS + s] = block
                blocks.append(block)
            columns = column_block(place_ref, owner, row, col_origin, starts)
            acc_ref[...] += times_stack(columns, jnp.concatenate(blocks, axis=1))

    ground = jnp.concatenate(
        [ground_ref[:, start : start + LANES] for start in starts], axis=1
    )
    depth = surface(acc_ref[...], mean, ground)
    depth_ref[...] = depth
    for out_ref, start, pick in ((left_ref, 0, 0), (right_ref, LANES, LANES - SWEEPS)):
        for k, values in enumerate((depth, ground)):
            out_ref[k * SWEEPS : (k + 1) * SWEEPS, :] = jnp.transpose(
                values[:, start : start + LANES]
            )[pick : pick + SWEEPS]


def inner_kernel(first_slot, place_ref, stack_ref, mean_ref, ground_ref, depth_ref, acc_ref):
    tile_columns = ground_ref.shape[1]
    owners = place_ref.shape[0]
    col_origin = (lax.axis_index("col") * tile_columns).astype(F32)
    acc_ref[...] = jnp.zeros_like(acc_ref)
    starts = tuple(range(LANES, tile_columns - LANES, LANES))

    @pl.loop(0, owners)
    def _(owner):
        for slot in range(MOST):
            columns = column_block(place_ref, owner, first_slot + slot * 8, col_origin, starts)
            stack = jnp.concatenate(
                [stack_ref[owner * (MOST * SEGS) + slot * SEGS + s] for s in range(SEGS)], axis=1
            )
            acc_ref[...] += times_stack(columns, stack)

    ground = ground_ref[:, LANES : tile_columns - LANES]
    depth_ref[...] = surface(acc_ref[...], mean_ref[0:1, 0:1], ground)


def paste(outer, inner):
    return jnp.concatenate([outer[:, :LANES], inner, outer[:, LANES:]], axis=1)


def strip_kernel(outer_ref, inner_ref, ground_ref, left_ref, right_ref, strip_ref):
    tile_rows, tile_columns = ground_ref.shape
    sides = jnp.concatenate(
        [left_ref[:SWEEPS], right_ref[:SWEEPS], left_ref[SWEEPS:], right_ref[SWEEPS:]], axis=0
    )
    sides = jnp.transpose(sides)
    row = 0
    for k in range(2):
        for first in (0, tile_rows - SWEEPS):
            rows = slice(first, first + SWEEPS)
            if k == 0:
                main = paste(outer_ref[rows, :], inner_ref[rows, :])
            else:
                main = ground_ref[rows, :]
            strip_ref[row : row + SWEEPS, :tile_columns] = main
            strip_ref[row : row + SWEEPS, tile_columns:] = jnp.concatenate(
                [
                    sides[rows, 2 * SWEEPS * k : 2 * SWEEPS * (k + 1)],
                    jnp.zeros((SWEEPS, LANES - 2 * SWEEPS), F32),
                ],
                axis=1,
            )
            row += SWEEPS


def neighbour_rows(strip_ref, row_count):
    me = lax.axis_index("row")
    block = 4 * SWEEPS
    above = pl.multiple_of(jnp.maximum(me - 1, 0) * block, block)
    below = pl.multiple_of(jnp.minimum(me + 1, row_count - 1) * block, block)
    above = strip_ref[pl.ds(above, block), :]
    below = strip_ref[pl.ds(below, block), :]
    return (
        above[SWEEPS : 2 * SWEEPS],
        below[:SWEEPS],
        above[3 * SWEEPS :],
        below[2 * SWEEPS : 3 * SWEEPS],
    )


def sweep_kernel(
    row_count,
    col_count,
    strip_ref,
    left_ref,
    right_ref,
    outer_ref,
    inner_ref,
    ground_ref,
    out_ref,
    height_ref,
    land_ref,
):
    tile_rows, tile_columns = ground_ref.shape
    pad_rows, pad_cols = 8, LANES
    rows, cols = height_ref.shape
    depth_up, depth_down, ground_up, ground_down = neighbour_rows(strip_ref, row_count)
    sides = jnp.transpose(jnp.concatenate([left_ref[...], right_ref[...]], axis=0))
    last = pad_rows + tile_rows
    for ref, up, down, k in (
        (height_ref, depth_up, depth_down, 0),
        (land_ref, ground_up, ground_down, SWEEPS),
    ):
        ref[:pad_rows, :] = jnp.zeros((pad_rows, cols), F32)
        ref[last:, :] = jnp.zeros((rows - last, cols), F32)
        inner = slice(pad_cols, pad_cols + tile_columns)
        if k == 0:
            ref[pad_rows:last, pad_cols : 2 * pad_cols] = outer_ref[:, :LANES]
            ref[pad_rows:last, 2 * pad_cols : cols - 2 * pad_cols] = inner_ref[...]
            ref[pad_rows:last, cols - 2 * pad_cols : cols - pad_cols] = outer_ref[:, LANES:]
        else:
            ref[pad_rows:last, inner] = ground_ref[...]
        ref[pad_rows - SWEEPS : pad_rows, inner] = up[:, :tile_columns]
        ref[last : last + SWEEPS, inner] = down[:, :tile_columns]
        blank = jnp.zeros((tile_rows, LANES - SWEEPS), F32)
        left = sides[:, k : k + SWEEPS]
        right = sides[:, 2 * SWEEPS + k : 3 * SWEEPS + k]
        ref[pad_rows:last, :pad_cols] = jnp.concatenate([blank, left], axis=1)
        ref[pad_rows:last, cols - pad_cols :] = jnp.concatenate([right, blank], axis=1)
        for first, corner in ((pad_rows - SWEEPS, up), (last, down)):
            corner = corner[:, tile_columns : tile_columns + 2 * SWEEPS]
            ref[first : first + SWEEPS, pad_cols - SWEEPS : pad_cols] = corner[:, :SWEEPS]
            ref[first : first + SWEEPS, cols - pad_cols : cols - pad_cols + SWEEPS] = corner[:, SWEEPS:]

    row_id = lax.broadcasted_iota(jnp.int32, (rows, cols), 0) + (
        lax.axis_index("row") * tile_rows - pad_rows
    )
    col_id = lax.broadcasted_iota(jnp.int32, (rows, cols), 1) + (
        lax.axis_index("col") * tile_columns - pad_cols
    )
    grid_rows, grid_cols = tile_rows * row_count, tile_columns * col_count
    land = land_ref[...]
    down = flow_gain / (1.0 + jnp.abs(land - pltpu.roll(land, rows - 1, 0)))
    right = flow_gain / (1.0 + jnp.abs(land - pltpu.roll(land, cols - 1, 1)))
    down = jnp.where((row_id >= 0) & (row_id < grid_rows - 1), down, 0.0)
    right = jnp.where((col_id >= 0) & (col_id < grid_cols - 1), right, 0.0)
    up = pltpu.roll(down, 1, 0)
    left = pltpu.roll(right, 1, 1)
    scale = 1.0 / (1.0 + up + down + left + right)
    up, down, left, right = up * scale, down * scale, left * scale, right * scale
    height = height_ref[...]
    for _ in range(SWEEPS):
        height = (
            height * scale
            + up * pltpu.roll(height, 1, 0)
            + down * pltpu.roll(height, rows - 1, 0)
            + left * pltpu.roll(height, 1, 1)
            + right * pltpu.roll(height, cols - 1, 1)
        )
    out_ref[...] = height[pad_rows : pad_rows + tile_rows, pad_cols : pad_cols + tile_columns]


def shift(values, axis, step):
    count = lax.axis_size(axis)
    return lax.ppermute(values, axis, [(i, (i + step) % count) for i in range(count)])


def body(
    ground_level_map,
    shoreline_altitude_entries,
    shoreline_piece_position,
    lake_panel_locations,
    spanned_patch_verticals,
):
    tile_rows, tile_columns = ground_level_map.shape
    col_count = lax.axis_size("col")
    row_count = lax.axis_size("row")
    records, _ = shoreline_altitude_entries.shape
    bodies, _ = spanned_patch_verticals.shape
    covers = spanned_patch_verticals.T
    first_slot = bodies * SEGS + bodies // 2
    hbm = pl.BlockSpec(memory_space=pltpu.HBM)

    parts = pl.pallas_call(
        pack_kernel,
        out_shape=jax.ShapeDtypeStruct((col_count, first_slot + MOST * 8, LANES), F32),
        in_specs=[smem(), hbm, hbm, hbm],
        out_specs=vmem(),
        scratch_shapes=[
            pltpu.VMEM((records // LANES, LANES), jnp.int32),
            pltpu.VMEM((records, LANES), F32),
            pltpu.VMEM(lake_panel_locations.shape, F32),
            pltpu.SMEM((col_count,), jnp.int32),
            pltpu.SemaphoreType.DMA((3,)),
        ],
        compiler_params=params(60 * 1024 * 1024),
    )(
        covers,
        shoreline_piece_position.reshape(records // LANES, LANES),
        shoreline_altitude_entries,
        lake_panel_locations,
    )
    parts = lax.all_to_all(parts, "col", 0, 0, tiled=True)

    slot_rows = MOST * SEGS + 8
    sums = pl.pallas_call(
        owner_kernel,
        out_shape=jax.ShapeDtypeStruct((col_count, slot_rows, LANES), F32),
        in_specs=[smem(), vmem()],
        out_specs=vmem(),
        scratch_shapes=[
            pltpu.VMEM((first_slot, LANES), F32),
            pltpu.SMEM((col_count,), jnp.int32),
        ],
        compiler_params=params(),
    )(covers, parts)
    sums = lax.all_to_all(sums, "col", 0, 0, tiled=True)

    half = 2 * LANES
    blocks = col_count * MOST * SEGS
    flops = 4 * tile_rows * half * blocks * LANES
    edge = jax.ShapeDtypeStruct((2 * SWEEPS, tile_rows), F32)
    outer, left, right, stack, mean = pl.pallas_call(
        functools.partial(outer_kernel, first_slot),
        out_shape=(
            jax.ShapeDtypeStruct((tile_rows, half), F32),
            edge,
            edge,
            jax.ShapeDtypeStruct((blocks, 2 * tile_rows, LANES), BF16),
            jax.ShapeDtypeStruct((8, LANES), F32),
        ),
        in_specs=[vmem()] * 3,
        out_specs=(vmem(),) * 5,
        scratch_shapes=[pltpu.VMEM((half, 2 * tile_rows), F32)],
        compiler_params=params(),
        cost_estimate=pl.CostEstimate(flops=flops, transcendentals=0, bytes_accessed=1 << 20),
    )(parts, sums, ground_level_map)
    from_left = shift(right, "col", 1)
    from_right = shift(left, "col", -1)
    inside = tile_columns - half
    inner = pl.pallas_call(
        functools.partial(inner_kernel, first_slot),
        out_shape=jax.ShapeDtypeStruct((tile_rows, inside), F32),
        in_specs=[vmem()] * 4,
        out_specs=vmem(),
        scratch_shapes=[pltpu.VMEM((inside, 2 * tile_rows), F32)],
        compiler_params=params(),
        cost_estimate=pl.CostEstimate(flops=flops, transcendentals=0, bytes_accessed=1 << 20),
    )(parts, stack, mean, ground_level_map)

    strips = pl.pallas_call(
        strip_kernel,
        out_shape=jax.ShapeDtypeStruct((4 * SWEEPS, tile_columns + LANES), F32),
        in_specs=[vmem()] * 5,
        out_specs=vmem(),
        compiler_params=params(),
    )(outer, inner, ground_level_map, from_left, from_right)
    strips = lax.all_gather(strips, "row", axis=0, tiled=True)

    scratch = pltpu.VMEM((tile_rows + 16, tile_columns + 2 * LANES), F32)
    return pl.pallas_call(
        functools.partial(sweep_kernel, row_count, col_count),
        out_shape=jax.ShapeDtypeStruct((tile_rows, tile_columns), F32),
        in_specs=[vmem()] * 6,
        out_specs=vmem(),
        scratch_shapes=[scratch, scratch],
        compiler_params=params(),
    )(strips, from_left, from_right, outer, inner, ground_level_map)


def solution(mesh):
    in_specs = (
        P("row", "col"),
        P(("row", "col"), None),
        P(("row", "col")),
        P(("row", "col"), None, None),
        P(("row", "col"), None),
    )
    out_specs = P("row", "col")
    return jax.shard_map(body, mesh=mesh, in_specs=in_specs, out_specs=out_specs, check_vma=False)
```

time: 79.8 us -> 64.9 us (0.81)
  blocking collectives: 5.43 us -> 37.4 us
  Pallas kernels: 36.1 us -> 20.8 us
  waiting for transfers between devices: 15.2 us -> 0.01 us
  starting transfers between devices: 19 us -> 4.78 us
  local copies, waits for them, and re-layouts: 3.37 us -> 1.63 us
    all_to_all x0 -> x2, blocking collectives: none -> 31.9 us  [the longest x1 21.1 us: body(): parts = lax.all_to_all(parts, 'col', 0, 0, tiled=True)]
    pallas_call x5 -> x4, Pallas kernels: 32.2 us -> 17.7 us  [the longest x1 8.61 us: body(): pl.pallas_call(functools.partial(outer_kernel, first_slot), out_shape=(ja...]
    all_to_all x3 -> x0, starting transfers between devices: 14.2 us -> none  [the longest x1 7.28 us: body(): parts = lax.all_to_all(parts, 'col', 0, 0, tiled=True)]
    all_to_all x3 -> x0, waiting for transfers between devices: 13.5 us -> none  [the longest x1 7.23 us: body(): parts = lax.all_to_all(parts, 'col', 0, 0, tiled=True)]
    unnamed x9 -> x6, local copies, waits for them, and re-layouts: 3.37 us -> 1.63 us
    ppermute x2, waiting for transfers between devices: 1.63 us -> 0.01 us  [shift(): lax.ppermute(values, axis, [(i, (i + step) % count) for i in range(count)])]
  transfers between devices with their start and end apart: 5 -> 2, of which waited for: 3 -> 0; matrix products, arithmetic and copies ran while one was open for 1% -> 0% of each run, Pallas kernels for 23% -> 9%
where the time goes in v2:
time: 64.9 us; the launch traced here: 64.6 us
  blocking collectives  37.4 us (58%)
  Pallas kernels  20.8 us (32%)
  starting transfers between devices  4.78 us (7%)
  local copies, waits for them, and re-layouts  1.63 us (3%)
    all_to_all x1, blocking collectives, body(): parts = lax.all_to_all(parts, 'col', 0, 0, tiled=True)  21.1 us
    all_to_all x1, blocking collectives, body(): sums = lax.all_to_all(sums, 'col', 0, 0, tiled=True)  10.7 us
    pallas_call x1, Pallas kernels, body(): pl.pallas_call(functools.partial(outer_kernel, first_slot), out_shape=(ja...  8.61 us
    all_gather x1, blocking collectives, body(): strips = lax.all_gather(strips, 'row', axis=0, tiled=True)  5.52 us
    pallas_call x1, Pallas kernels, body(): pl.pallas_call(functools.partial(inner_kernel, first_slot), out_shape=jax...  5.51 us
    ppermute x2, starting transfers between devices, shift(): lax.ppermute(values, axis, [(i, (i + step) % count) for i in range(count)])  4.78 us
    pallas_call x1, Pallas kernels, body(): pl.pallas_call(pack_kernel, out_shape=jax.ShapeDtypeStruct((col_count, fi...  3.41 us
    pallas_call x1, Pallas kernels, body(): pl.pallas_call(functools.partial(sweep_kernel, row_count, col_count), out...  2.4 us
  transfers between devices with their start and end apart: 2, of which 0 were waited for; matrix products, arithmetic and copies ran while one was open for 0% of the time, Pallas kernels for 9%

profile of v2, /device:TPU:0, one launch (start us, length us, event | category | flops | bytes accessed | tf_op | source)
XLA Modules:
  0.0 64.6 jit_solution(13830525056039505673)
XLA Ops:
  0.0 3.4 %shard_map.55 = f32[8,120,128]{2,1,0:T(8,128)} custom-call(s32[2,16]{1,0:T(2,128)} %bitcast.2, s32[8,128]{1,0:T(8,128)} %bitcast.4, f32[1024,128]{1,0:T(8,128)} %entry_hbm.1, f32[16,2,512]{2,1,0:T(2,128)} %place_hbm.1), custom_call_target="tpu_custom_call" | custom-call | tf_op jit(solution)/shard_map/pallas_call | solution.py:370
  3.4 21.1 %all_to_all.10.part_ref.place_ref = f32[8,120,128]{2,1,0:T(8,128)S(1)} all-to-all(f32[8,120,128]{2,1,0:T(8,128)} %shard_map.55), channel_id=1, replica_groups=mesh['row'=4,'col'=8] {'col'}, dimensions={0} | all-to-all | bytes 983040 | tf_op jit(solution)/shard_map/all_to_all | solution.py:389
  24.5 0.0 copy-start.2
  24.5 0.7 %copy-done.2 = s32[16,2]{0,1:T(2,128)S(1)} copy-done((s32[16,2]{0,1:T(2,128)S(1)}, s32[16,2]{0,1:T(2,128)}, u32[]{:S(2)}) %copy-start.2) | copy-done | bytes 152
  25.2 0.7 %shard_map.56 = f32[8,32,128]{2,1,0:T(8,128)S(1)} custom-call(s32[2,16]{1,0:T(2,128)S(1)} %bitcast.3, f32[8,120,128]{2,1,0:T(8,128)S(1)} %all_to_all.10.part_ref.place_ref), custom_call_target="tpu_custom_call" | custom-call | tf_op jit(solution)/shard_map/pallas_call | solution.py:392
  25.9 10.7 %all_to_all.11.sums_ref = f32[8,32,128]{2,1,0:T(8,128)S(1)} all-to-all(f32[8,32,128]{2,1,0:T(8,128)S(1)} %shard_map.56), channel_id=1, replica_groups=mesh['row'=4,'col'=8] {'col'}, dimensions={0} | all-to-all | bytes 262144 | tf_op jit(solution)/shard_map/all_to_all | solution.py:403
  36.7 0.0 copy-start
  36.7 0.9 %copy-done = f32[128,512]{1,0:T(8,128)S(1)} copy-done((f32[128,512]{1,0:T(8,128)S(1)}, f32[128,512]{1,0:T(8,128)}, u32[]{:S(2)}) %copy-start) | copy-done | bytes 262168
  37.6 0.0 copy-start.1
  37.6 8.6 %shard_map.57 = (f32[128,256]{1,0:T(8,128)S(1)}, f32[8,128]{1,0:T(8,128)S(1)}, f32[8,128]{1,0:T(8,128)S(1)}, bf16[192,256,128]{2,1,0:T(8,128)(2,1)S(1)}, f32[8,128]{1,0:T(8,128)S(1)}) custom-call(f32[8,120,128]{2,1,0:T(8,128)S(1)} %all_to_all.10.part_ref.place_ref, f32[8,32,128]{2,1,0:T(8,128)S(1)} %all_to_all.11.sums_ref, f32[128,512]{1,0:T(8,128)S(1)} %copy-done), custom_call_target="tpu_custom_call" | custom-call | flops 3221225472 | bytes 1048576 | tf_op jit(solution)/shard_map/pallas_call | solution.py:409
  46.2 0.3 collective-permute-start
  46.5 4.5 %collective-permute-start.1 = (f32[8,128]{1,0:T(8,128)S(1)}, f32[8,128]{1,0:T(8,128)S(1)}, u32[]{:S(2)}, u32[]{:S(2)}) collective-permute-start(f32[8,128]{1,0:T(8,128)S(1)} %get-tuple-element.14), channel_id=1, source_target_pairs={{0,7},{1,0},{2,1},{3,2},{4,3},{5,4},{6,5},{7,6},{8,15},{9,8},{10,9... | collective-permute-start | bytes 12296 | tf_op jit(solution)/shard_map/ppermute | solution.py:351
  51.0 5.5 %shard_map.58.inner_ref = f32[128,256]{1,0:T(8,128)S(1)} custom-call(f32[8,120,128]{2,1,0:T(8,128)S(1)} %all_to_all.10.part_ref.place_ref, bf16[192,256,128]{2,1,0:T(8,128)(2,1)S(1)} %get-tuple-element.11.stack_ref, f32[8,128]{1,0:T(8,128)S(1)} %get-tuple-element.12.mean_ref, f32[128,512]{1,0:T(8,128)S(1)} %copy-done), custom_call_target="tpu_custom_call" | custom-call | flops 3221225472 | bytes 1048576 | tf_op jit(solution)/shard_map/pallas_call | solution.py:427
  56.5 0.0 collective-permute-done.left_ref
  56.5 0.0 collective-permute-done.1.right_ref
  56.5 0.2 shard_map.59
  56.7 5.5 %all_gather.3.strip_ref = f32[64,640]{1,0:T(8,128)S(1)} all-gather(f32[16,640]{1,0:T(8,128)S(1)} %shard_map.59), channel_id=1, replica_groups=mesh['row'=4,'col'=8] {'row'}, dimensions={0}, use_global_device_ids=true | all-gather | bytes 204800 | tf_op jit(solution)/shard_map/all_gather | solution.py:444
  62.2 0.0 copy-done.1
  62.2 2.4 %shard_map.60 = f32[128,512]{1,0:T(8,128)} custom-call(f32[64,640]{1,0:T(8,128)S(1)} %all_gather.3.strip_ref, f32[8,128]{1,0:T(8,128)S(1)} %collective-permute-done.left_ref, f32[8,128]{1,0:T(8,128)S(1)} %collective-permute-done.1.right_ref, f32[128,256]{1,0:T(8,128)S(1)} %get-tuple-element.10.outer_ref, f32[128,256]{1,0:T(8,128)S(1)} %shard_map.58.inner_ref, ...), custom_call_target="tpu_custom_call" | custom-call | tf_op jit(solution)/shard_map/pallas_call | solution.py:447
Async XLA Ops:
  24.5 0.7 %copy-start.2 = (s32[16,2]{0,1:T(2,128)S(1)}, s32[16,2]{0,1:T(2,128)}, u32[]{:S(2)}) copy-start(s32[16,2]{0,1:T(2,128)} %param.9) | copy-start | bytes 388
  36.7 1.0 %copy-start = (f32[128,512]{1,0:T(8,128)S(1)}, f32[128,512]{1,0:T(8,128)}, u32[]{:S(2)}) copy-start(f32[128,512]{1,0:T(8,128)} %ground_ref.7) | copy-start | bytes 786436
  37.6 24.6 %copy-start.1 = (f32[128,512]{1,0:T(8,128)S(1)}, f32[128,512]{1,0:T(8,128)}, u32[]{:S(2)}) copy-start(f32[128,512]{1,0:T(8,128)} %ground_ref.7) | copy-start | bytes 786436
  46.2 10.3 %collective-permute-start = (f32[8,128]{1,0:T(8,128)S(1)}, f32[8,128]{1,0:T(8,128)S(1)}, u32[]{:S(2)}, u32[]{:S(2)}) collective-permute-start(f32[8,128]{1,0:T(8,128)S(1)} %get-tuple-element.13), channel_id=1, source_target_pairs={{0,1},{1,2},{2,3},{3,4},{4,5},{5,6},{6,7},{7,0},{8,9},{9,10},{10,1... | collective-permute-start | bytes 12296 | tf_op jit(solution)/shard_map/ppermute | solution.py:351
  46.5 10.0 %collective-permute-start.1 = (f32[8,128]{1,0:T(8,128)S(1)}, f32[8,128]{1,0:T(8,128)S(1)}, u32[]{:S(2)}, u32[]{:S(2)}) collective-permute-start(f32[8,128]{1,0:T(8,128)S(1)} %get-tuple-element.14), channel_id=1, source_target_pairs={{0,7},{1,0},{2,1},{3,2},{4,3},{5,4},{6,5},{7,6},{8,15},{9,8},{10,9... | collective-permute-start | bytes 12296 | tf_op jit(solution)/shard_map/ppermute | solution.py:351

commit v3 on v2

--- a/solution.py
+++ b/solution.py
@@ -37,13 +37,35 @@
     return jnp.where(cond, 1.0, 0.0).astype(BF16)
 
 
-def pack_kernel(cover_ref, ids_hbm, entry_hbm, place_hbm, out_ref, ids_ref, entry_ref, place_ref, used_ref, sems):
+def pack_kernel(
+    cover_hbm,
+    ids_hbm,
+    entry_hbm,
+    place_hbm,
+    ground_hbm,
+    out_ref,
+    ground_ref,
+    cover_copy_ref,
+    cover_ref,
+    ids_ref,
+    entry_ref,
+    place_ref,
+    used_ref,
+    sems,
+):
     owners, _, _ = out_ref.shape
     covers, bodies = cover_ref.shape
     copies = [
         pltpu.make_async_copy(source, target, sems.at[k])
         for k, (source, target) in enumerate(
-            ((ids_hbm, ids_ref), (entry_hbm, entry_ref), (place_hbm, place_ref))
+            (
+                (ids_hbm, ids_ref),
+                (entry_hbm, entry_ref),
+                (place_hbm, place_ref),
+                (cover_hbm, cover_ref),
+                (cover_hbm, cover_copy_ref),
+                (ground_hbm, ground_ref),
+            )
         )
     ]
     for copy in copies:
@@ -52,7 +74,8 @@
     sum_rows, count_rows = bodies * SEGS, bodies // 2
     first_slot = sum_rows + count_rows
     out_ref[:, first_slot:, :] = jnp.zeros((owners, MOST * 8, LANES), F32)
-    copies[0].wait()
+    for copy in copies:
+        copy.wait()
     seg_iota = lax.broadcasted_iota(jnp.int32, (owners * sum_rows, LANES), 0)
     pair_iota = lax.broadcasted_iota(jnp.int32, (owners * count_rows, LANES), 0)
     lane_group = lax.broadcasted_iota(jnp.int32, (LANES, LANES), 0) // 16
@@ -63,7 +86,6 @@
         by_pair, by_lane, (((1,), (1,)), ((), ())), preferred_element_type=F32
     )
     by_segment = jnp.concatenate([one_hot(seg_iota == v) for v in ids], axis=1)
-    copies[1].wait()
     entries = entry_ref[...]
     high = entries.astype(BF16)
     low = (entries - high.astype(F32)).astype(BF16)
@@ -76,7 +98,6 @@
         out_ref[owner, sum_rows:first_slot, :] = counts[
             owner * count_rows : (owner + 1) * count_rows
         ]
-    copies[2].wait()
     for column in range(owners):
         used_ref[column] = 0
     for body_id in range(bodies):
@@ -288,48 +309,47 @@
     land_ref,
 ):
     tile_rows, tile_columns = ground_ref.shape
-    pad_rows, pad_cols = 8, LANES
     rows, cols = height_ref.shape
     depth_up, depth_down, ground_up, ground_down = neighbour_rows(strip_ref, row_count)
     sides = jnp.transpose(jnp.concatenate([left_ref[...], right_ref[...]], axis=0))
-    last = pad_rows + tile_rows
+    blank = cols - tile_columns - 2 * SWEEPS
+
+    def spare(left, right):
+        return jnp.concatenate([right, jnp.zeros((right.shape[0], blank), F32), left], axis=1)
+
     for ref, up, down, k in (
         (height_ref, depth_up, depth_down, 0),
         (land_ref, ground_up, ground_down, SWEEPS),
     ):
-        ref[:pad_rows, :] = jnp.zeros((pad_rows, cols), F32)
-        ref[last:, :] = jnp.zeros((rows - last, cols), F32)
-        inner = slice(pad_cols, pad_cols + tile_columns)
         if k == 0:
-            ref[pad_rows:last, pad_cols : 2 * pad_cols] = outer_ref[:, :LANES]
-            ref[pad_rows:last, 2 * pad_cols : cols - 2 * pad_cols] = inner_ref[...]
-            ref[pad_rows:last, cols - 2 * pad_cols : cols - pad_cols] = outer_ref[:, LANES:]
+            ref[:tile_rows, :LANES] = outer_ref[:, :LANES]
+            ref[:tile_rows, LANES : tile_columns - LANES] = inner_ref[...]
+            ref[:tile_rows, tile_columns - LANES : tile_columns] = outer_ref[:, LANES:]
         else:
-            ref[pad_rows:last, inner] = ground_ref[...]
-        ref[pad_rows - SWEEPS : pad_rows, inner] = up[:, :tile_columns]
-        ref[last : last + SWEEPS, inner] = down[:, :tile_columns]
-        blank = jnp.zeros((tile_rows, LANES - SWEEPS), F32)
+            ref[:tile_rows, :tile_columns] = ground_ref[...]
+        ref[tile_rows:, :tile_columns] = jnp.concatenate(
+            [down[:, :tile_columns], up[:, :tile_columns]], axis=0
+        )
         left = sides[:, k : k + SWEEPS]
         right = sides[:, 2 * SWEEPS + k : 3 * SWEEPS + k]
-        ref[pad_rows:last, :pad_cols] = jnp.concatenate([blank, left], axis=1)
-        ref[pad_rows:last, cols - pad_cols :] = jnp.concatenate([right, blank], axis=1)
-        for first, corner in ((pad_rows - SWEEPS, up), (last, down)):
-            corner = corner[:, tile_columns : tile_columns + 2 * SWEEPS]
-            ref[first : first + SWEEPS, pad_cols - SWEEPS : pad_cols] = corner[:, :SWEEPS]
-            ref[first : first + SWEEPS, cols - pad_cols : cols - pad_cols + SWEEPS] = corner[:, SWEEPS:]
-
-    row_id = lax.broadcasted_iota(jnp.int32, (rows, cols), 0) + (
-        lax.axis_index("row") * tile_rows - pad_rows
-    )
-    col_id = lax.broadcasted_iota(jnp.int32, (rows, cols), 1) + (
-        lax.axis_index("col") * tile_columns - pad_cols
-    )
+        ref[:tile_rows, tile_columns:] = spare(left, right)
+        corner = jnp.concatenate([down[:, tile_columns:], up[:, tile_columns:]], axis=0)
+        ref[tile_rows:, tile_columns:] = spare(
+            corner[:, :SWEEPS], corner[:, SWEEPS : 2 * SWEEPS]
+        )
+
+    row_id = lax.broadcasted_iota(jnp.int32, (rows, 1), 0)
+    row_id = jnp.where(row_id < tile_rows + SWEEPS, row_id, row_id - rows)
+    row_id = row_id + lax.axis_index("row") * tile_rows
+    col_id = lax.broadcasted_iota(jnp.int32, (1, cols), 1)
+    col_id = jnp.where(col_id < tile_columns + LANES // 2, col_id, col_id - cols)
+    col_id = col_id + lax.axis_index("col") * tile_columns
     grid_rows, grid_cols = tile_rows * row_count, tile_columns * col_count
     land = land_ref[...]
-    down = flow_gain / (1.0 + jnp.abs(land - pltpu.roll(land, rows - 1, 0)))
-    right = flow_gain / (1.0 + jnp.abs(land - pltpu.roll(land, cols - 1, 1)))
-    down = jnp.where((row_id >= 0) & (row_id < grid_rows - 1), down, 0.0)
-    right = jnp.where((col_id >= 0) & (col_id < grid_cols - 1), right, 0.0)
+    gain_down = jnp.where((row_id >= 0) & (row_id < grid_rows - 1), flow_gain, 0.0)
+    gain_right = jnp.where((col_id >= 0) & (col_id < grid_cols - 1), flow_gain, 0.0)
+    down = gain_down / (1.0 + jnp.abs(land - pltpu.roll(land, rows - 1, 0)))
+    right = gain_right / (1.0 + jnp.abs(land - pltpu.roll(land, cols - 1, 1)))
     up = pltpu.roll(down, 1, 0)
     left = pltpu.roll(right, 1, 1)
     scale = 1.0 / (1.0 + up + down + left + right)
@@ -343,7 +363,7 @@
             + left * pltpu.roll(height, 1, 1)
             + right * pltpu.roll(height, cols - 1, 1)
         )
-    out_ref[...] = height[pad_rows : pad_rows + tile_rows, pad_cols : pad_cols + tile_columns]
+    out_ref[...] = height[:tile_rows, :tile_columns]
 
 
 def shift(values, axis, step):
@@ -367,24 +387,35 @@
     first_slot = bodies * SEGS + bodies // 2
     hbm = pl.BlockSpec(memory_space=pltpu.HBM)
 
-    parts = pl.pallas_call(
+    parts, ground_level_map, covers = pl.pallas_call(
         pack_kernel,
-        out_shape=jax.ShapeDtypeStruct((col_count, first_slot + MOST * 8, LANES), F32),
-        in_specs=[smem(), hbm, hbm, hbm],
-        out_specs=vmem(),
+        out_shape=(
+            jax.ShapeDtypeStruct((col_count, first_slot + MOST * 8, LANES), F32),
+            jax.ShapeDtypeStruct(ground_level_map.shape, F32),
+            jax.ShapeDtypeStruct(covers.shape, jnp.int32),
+        ),
+        in_specs=[hbm] * 5,
+        out_specs=(vmem(),) * 3,
         scratch_shapes=[
+            pltpu.SMEM(covers.shape, jnp.int32),
             pltpu.VMEM((records // LANES, LANES), jnp.int32),
             pltpu.VMEM((records, LANES), F32),
             pltpu.VMEM(lake_panel_locations.shape, F32),
             pltpu.SMEM((col_count,), jnp.int32),
-            pltpu.SemaphoreType.DMA((3,)),
+            pltpu.SemaphoreType.DMA((6,)),
         ],
-        compiler_params=params(60 * 1024 * 1024),
+        compiler_params=params(),
     )(
-        covers,
-        shoreline_piece_position.reshape(records // LANES, LANES),
-        shoreline_altitude_entries,
-        lake_panel_locations,
+        *(
+            pltpu.with_memory_space_constraint(value, pltpu.HBM)
+            for value in (
+                covers,
+                shoreline_piece_position.reshape(records // LANES, LANES),
+                shoreline_altitude_entries,
+                lake_panel_locations,
+                ground_level_map,
+            )
+        )
     )
     parts = lax.all_to_all(parts, "col", 0, 0, tiled=True)
 
@@ -443,7 +474,7 @@
     )(outer, inner, ground_level_map, from_left, from_right)
     strips = lax.all_gather(strips, "row", axis=0, tiled=True)
 
-    scratch = pltpu.VMEM((tile_rows + 16, tile_columns + 2 * LANES), F32)
+    scratch = pltpu.VMEM((tile_rows + 2 * SWEEPS, tile_columns + LANES), F32)
     return pl.pallas_call(
         functools.partial(sweep_kernel, row_count, col_count),
         out_shape=jax.ShapeDtypeStruct((tile_rows, tile_columns), F32),

time: 64.9 us -> 61 us (0.940)
  Pallas kernels: 20.8 us -> 18.7 us
  local copies, waits for them, and re-layouts: 1.63 us -> 0 us
    pallas_call x1, Pallas kernels: 3.41 us -> 1.76 us  [body(): pl.pallas_call(pack_kernel, out_shape=(jax.ShapeDtypeStruct((col_count, f...]
    unnamed x6 -> x0, local copies, waits for them, and re-layouts: 1.63 us -> none
where the time goes in v3:
time: 61 us; the launch traced here: 60.7 us
  blocking collectives  37.2 us (61%)
  Pallas kernels  18.7 us (31%)
  starting transfers between devices  4.78 us (8%)
    all_to_all x1, blocking collectives, body(): parts = lax.all_to_all(parts, 'col', 0, 0, tiled=True)  20.9 us
    all_to_all x1, blocking collectives, body(): sums = lax.all_to_all(sums, 'col', 0, 0, tiled=True)  10.7 us
    pallas_call x1, Pallas kernels, body(): pl.pallas_call(functools.partial(outer_kernel, first_slot), out_shape=(ja...  8.61 us
    all_gather x1, blocking collectives, body(): strips = lax.all_gather(strips, 'row', axis=0, tiled=True)  5.52 us
    pallas_call x1, Pallas kernels, body(): pl.pallas_call(functools.partial(inner_kernel, first_slot), out_shape=jax...  5.5 us
    ppermute x2, starting transfers between devices, shift(): lax.ppermute(values, axis, [(i, (i + step) % count) for i in range(count)])  4.78 us
    pallas_call x1, Pallas kernels, body(): pl.pallas_call(functools.partial(sweep_kernel, row_count, col_count), out...  2 us
    pallas_call x1, Pallas kernels, body(): pl.pallas_call(pack_kernel, out_shape=(jax.ShapeDtypeStruct((col_count, f...  1.76 us
  transfers between devices with their start and end apart: 2, of which 0 were waited for; matrix products, arithmetic and copies ran while one was open for 0% of the time, Pallas kernels for 9%

profile of v3, /device:TPU:0, one launch (start us, length us, event | category | flops | bytes accessed | tf_op | source)
XLA Modules:
  0.0 60.7 jit_solution(18103291866420026850)
XLA Ops:
  0.0 1.8 %shard_map.55 = (f32[8,120,128]{2,1,0:T(8,128)S(1)}, f32[128,512]{1,0:T(8,128)S(1)}, s32[2,16]{1,0:T(2,128)S(1)}) custom-call(s32[2,16]{1,0:T(2,128)} %bitcast.3, s32[8,128]{1,0:T(8,128)} %bitcast.2, f32[1024,128]{1,0:T(8,128)} %entry_hbm.1, f32[16,2,512]{2,1,0:T(2,128)} %place_hbm.1, f32[128,512]{1,0:T(8,128)} %ground_hbm.1), custom_call_target="tpu_custom_call" | custom-call | tf_op jit(solution)/shard_map/pallas_call | solution.py:390
  1.8 20.9 %all_to_all.10.part_ref.place_ref = f32[8,120,128]{2,1,0:T(8,128)S(1)} all-to-all(f32[8,120,128]{2,1,0:T(8,128)S(1)} %get-tuple-element.13), channel_id=1, replica_groups=mesh['row'=4,'col'=8] {'col'}, dimensions={0} | all-to-all | bytes 983040 | tf_op jit(solution)/shard_map/all_to_all | solution.py:420
  22.7 0.7 %shard_map.56 = f32[8,32,128]{2,1,0:T(8,128)S(1)} custom-call(s32[2,16]{1,0:T(2,128)S(1)} %get-tuple-element.14.cover_ref, f32[8,120,128]{2,1,0:T(8,128)S(1)} %all_to_all.10.part_ref.place_ref), custom_call_target="tpu_custom_call" | custom-call | tf_op jit(solution)/shard_map/pallas_call | solution.py:423
  23.4 10.7 %all_to_all.11.sums_ref = f32[8,32,128]{2,1,0:T(8,128)S(1)} all-to-all(f32[8,32,128]{2,1,0:T(8,128)S(1)} %shard_map.56), channel_id=1, replica_groups=mesh['row'=4,'col'=8] {'col'}, dimensions={0} | all-to-all | bytes 262144 | tf_op jit(solution)/shard_map/all_to_all | solution.py:434
  34.1 8.6 %shard_map.57 = (f32[128,256]{1,0:T(8,128)S(1)}, f32[8,128]{1,0:T(8,128)S(1)}, f32[8,128]{1,0:T(8,128)S(1)}, bf16[192,256,128]{2,1,0:T(8,128)(2,1)S(1)}, f32[8,128]{1,0:T(8,128)S(1)}) custom-call(f32[8,120,128]{2,1,0:T(8,128)S(1)} %all_to_all.10.part_ref.place_ref, f32[8,32,128]{2,1,0:T(8,128)S(1)} %all_to_all.11.sums_ref, ...), custom_call_target="tpu_custom_call" | custom-call | flops 3221225472 | bytes 1048576 | tf_op jit(solution)/shard_map/pallas_call | solution.py:440
  42.8 0.3 collective-permute-start
  43.0 4.5 %collective-permute-start.1 = (f32[8,128]{1,0:T(8,128)S(1)}, f32[8,128]{1,0:T(8,128)S(1)}, u32[]{:S(2)}, u32[]{:S(2)}) collective-permute-start(f32[8,128]{1,0:T(8,128)S(1)} %get-tuple-element.20), channel_id=1, source_target_pairs={{0,7},{1,0},{2,1},{3,2},{4,3},{5,4},{6,5},{7,6},{8,15},{9,8},{10,9... | collective-permute-start | bytes 12296 | tf_op jit(solution)/shard_map/ppermute | solution.py:371
  47.5 5.5 %shard_map.58.inner_ref = f32[128,256]{1,0:T(8,128)S(1)} custom-call(f32[8,120,128]{2,1,0:T(8,128)S(1)} %all_to_all.10.part_ref.place_ref, bf16[192,256,128]{2,1,0:T(8,128)(2,1)S(1)} %get-tuple-element.17.stack_ref, f32[8,128]{1,0:T(8,128)S(1)} %get-tuple-element.18.mean_ref, f32[128,512]{1,0:T(8,128)S(1)} %get-tuple-element.15.ground_ref), custom_call_target="tpu_custom_call" | custom-call | flops 3221225472 | bytes 1048576 | tf_op jit(solution)/shard_map/pallas_call | solution.py:458
  53.0 0.0 collective-permute-done.left_ref
  53.1 0.0 collective-permute-done.1.right_ref
  53.1 0.2 shard_map.59
  53.2 5.5 %all_gather.3.strip_ref = f32[64,640]{1,0:T(8,128)S(1)} all-gather(f32[16,640]{1,0:T(8,128)S(1)} %shard_map.59), channel_id=1, replica_groups=mesh['row'=4,'col'=8] {'row'}, dimensions={0}, use_global_device_ids=true | all-gather | bytes 204800 | tf_op jit(solution)/shard_map/all_gather | solution.py:475
  58.7 2.0 %shard_map.60 = f32[128,512]{1,0:T(8,128)} custom-call(f32[64,640]{1,0:T(8,128)S(1)} %all_gather.3.strip_ref, f32[8,128]{1,0:T(8,128)S(1)} %collective-permute-done.left_ref, f32[8,128]{1,0:T(8,128)S(1)} %collective-permute-done.1.right_ref, f32[128,256]{1,0:T(8,128)S(1)} %get-tuple-element.16.outer_ref, f32[128,256]{1,0:T(8,128)S(1)} %shard_map.58.inner_ref, ...), custom_call_target="tpu_custom_call" | custom-call | tf_op jit(solution)/shard_map/pallas_call | solution.py:478
Async XLA Ops:
  42.8 10.3 %collective-permute-start = (f32[8,128]{1,0:T(8,128)S(1)}, f32[8,128]{1,0:T(8,128)S(1)}, u32[]{:S(2)}, u32[]{:S(2)}) collective-permute-start(f32[8,128]{1,0:T(8,128)S(1)} %get-tuple-element.19), channel_id=1, source_target_pairs={{0,1},{1,2},{2,3},{3,4},{4,5},{5,6},{6,7},{7,0},{8,9},{9,10},{10,1... | collective-permute-start | bytes 12296 | tf_op jit(solution)/shard_map/ppermute | solution.py:371
  43.0 10.0 %collective-permute-start.1 = (f32[8,128]{1,0:T(8,128)S(1)}, f32[8,128]{1,0:T(8,128)S(1)}, u32[]{:S(2)}, u32[]{:S(2)}) collective-permute-start(f32[8,128]{1,0:T(8,128)S(1)} %get-tuple-element.20), channel_id=1, source_target_pairs={{0,7},{1,0},{2,1},{3,2},{4,3},{5,4},{6,5},{7,6},{8,15},{9,8},{10,9... | collective-permute-start | bytes 12296 | tf_op jit(solution)/shard_map/ppermute | solution.py:371
